TPU v7x, 256 devices: a whole 4x4x8 slice. The times are simulated.
256 devices in a mesh: leaf: 8 (over z), row: 2 (over core), col: 16 (over y, x).
Axes of the slice: x: 4, y: 4, z: 8, core: 2. Of those that a mesh axis runs over, the one named last changes fastest.
Arguments:
- front_tiles: bfloat16 [8, 2, 16, 2, 128, 2, 16, 2, 128], P('leaf', None, None, 'row', None, None, 'col'), as said below
- regular: float32 [8, 2, 16, 2, 128], P('leaf', None, 'col', 'row'), may hold values from 0.25 to 2.5
- child_map: int32 [8, 62], P('leaf'), may hold values from 0 to 63, as said below
Outputs:
- panel_factor: float32 [8, 2, 16, 2, 128, 256], P('leaf', None, None, 'row', None, 'col')
- parent_update: float32 [8, 1, 16, 2, 128, 2, 16, 2, 128], P('leaf', None, None, 'row', None, None, 'col')
Inputs may be any that keep to these rules, and one draw needn't show every extreme that they name: Each leaf's front_tiles form a symmetric positive semidefinite matrix, the product of a block-sparse constraint matrix (2 of 16 variable blocks per block row), a positive diagonal and its transpose; blocks that share no variable block are zero. `child_map`: within a leaf the entries are strictly increasing.
All inputs are finite; a program needn't handle non-finite values.
Results may differ from a plain program's by a relative error of at most 0.0016.
Values may be sent and summed in bfloat16 or wider, within the bound.
A program may use at most 128 MiB of HBM per device.

v0:
```python
import jax
import jax.numpy as jnp
from jax import lax
from jax.sharding import PartitionSpec as P

NPAN = 1


def broadcast(block, axis, source):
    block = jnp.where(lax.axis_index(axis) == source, block, jnp.zeros_like(block))
    return lax.psum(block, axis)


def passed_along(array, axis, by):
    length = lax.axis_size(axis)
    return lax.ppermute(array, axis, [(i, (i + by) % length) for i in range(length)])


def swapped(value, axis, bit):
    mask = 2**bit
    pairs = [(source, source ^ mask) for source in range(lax.axis_size(axis))]
    return lax.ppermute(value, axis, pairs)


def regularized(tiles, regular_local, col_at, row_at):
    shape = tiles.shape
    outer_ids = lax.broadcasted_iota(jnp.int32, shape, 0)
    col_ids = lax.broadcasted_iota(jnp.int32, shape, 1)
    cell_ids = lax.broadcasted_iota(jnp.int32, shape, 2)
    other_outer = lax.broadcasted_iota(jnp.int32, shape, 3)
    row_ids = lax.broadcasted_iota(jnp.int32, shape, 4)
    other_cell = lax.broadcasted_iota(jnp.int32, shape, 5)
    on_diagonal = (
        (outer_ids == other_outer)
        & (col_ids == col_at)
        & (row_ids == row_at)
        & (cell_ids == other_cell)
    )
    gains = regular_local[:, None, :, None, None, None]
    return tiles.astype(jnp.float32) + jnp.where(on_diagonal, gains, 0.0)


def shards(front_tiles, regular, child_map):
    row_count = lax.axis_size("row")
    col_count = lax.axis_size("col")
    row_at = lax.axis_index("row")
    col_at = lax.axis_index("col")
    tile_size = front_tiles.shape[-1]
    local_outer = front_tiles.shape[1]
    rows_local = local_outer * col_count * tile_size
    cols_local = local_outer * row_count * tile_size
    panel_width = row_count * tile_size
    highest = lax.Precision.HIGHEST
    front_six = front_tiles.reshape(
        local_outer, col_count, tile_size, local_outer, row_count, tile_size
    )
    regular_local = regular.reshape(local_outer, tile_size)
    local_panel = regularized(front_six[:, :, :, :1], regular_local, col_at, row_at).reshape(
        rows_local, panel_width
    )
    slab_cols = broadcast(local_panel, "col", 0)
    corner = lax.all_gather(slab_cols[0 * tile_size : 1 * tile_size], "row", axis=0, tiled=True)
    factor = jnp.linalg.cholesky(corner)
    solved = jax.scipy.linalg.solve_triangular(factor, slab_cols[tile_size:].T, lower=True).T
    own_rows = lax.dynamic_slice_in_dim(factor, row_at * tile_size, tile_size, 0)
    rows_part = jnp.concatenate(
        [jnp.zeros((0, panel_width), jnp.float32), own_rows, solved], axis=0
    )
    chosen = lax.dynamic_index_in_dim(
        rows_part.reshape(local_outer, col_count, tile_size, panel_width), col_at, 1, keepdims=False
    )
    cols_part = lax.all_gather(chosen[:, None], "row", axis=1, tiled=True).reshape(
        cols_local, panel_width
    )
    done = [(rows_part, cols_part)]
    all_panels = jnp.concatenate([pair[0] for pair in done], axis=1)
    all_cols = jnp.concatenate([pair[1] for pair in done], axis=1)
    schur_block = regularized(front_six, regular_local, col_at, row_at).reshape(
        rows_local, cols_local
    )
    schur_block = schur_block - jnp.einsum("ik,jk->ij", all_panels, all_cols, precision=highest)
    out_width = NPAN * panel_width // col_count
    factor_out = lax.dynamic_slice_in_dim(all_panels, col_at * out_width, out_width, 1)
    factor_out = factor_out.reshape(1, local_outer, col_count, 1, tile_size, out_width)
    targets = child_map.reshape(-1)
    child_blocks = targets.shape[0]
    panel_blocks = NPAN * row_count
    child_range = jnp.arange(child_blocks, dtype=jnp.int32)

    def source_of(parent_ids):
        matches = targets[None, :] == parent_ids[:, None]
        present = jnp.any(matches, axis=1)
        source_ids = panel_blocks + jnp.sum(jnp.where(matches, child_range[None, :], 0), axis=1)
        return (present, source_ids)

    low_block = schur_block.astype(jnp.bfloat16).reshape(1, rows_local, cols_local)
    every_rows = lax.all_gather(low_block, "row", axis=0, tiled=True)
    every_rows = every_rows.reshape(row_count * local_outer * col_count, tile_size, cols_local)
    outer_ids = jnp.arange(local_outer, dtype=jnp.int32)
    row_parents = (
        (outer_ids[:, None] * col_count + jnp.arange(col_count, dtype=jnp.int32)[None, :])
        * row_count
        + row_at
    ).reshape(-1)
    row_present, row_source = source_of(row_parents)
    row_index = (
        row_source % row_count * (local_outer * col_count)
        + row_source // (row_count * col_count) * col_count
        + row_source // row_count % col_count
    )
    row_index = jnp.where(row_present, row_index, 0)
    routed_rows = jnp.take(every_rows, row_index, axis=0)
    routed_rows = jnp.where(row_present[:, None, None], routed_rows, jnp.zeros_like(routed_rows))
    routed_rows = routed_rows.reshape(rows_local, local_outer * row_count, tile_size)
    candidates = [routed_rows]
    candidates.append(passed_along(routed_rows, "col", -1))
    stacked = jnp.concatenate(candidates, axis=1)
    col_parents = (
        (outer_ids[:, None] * col_count + col_at) * row_count
        + jnp.arange(row_count, dtype=jnp.int32)[None, :]
    ).reshape(-1)
    col_present, col_source = source_of(col_parents)
    reach_ids = col_source // row_count - col_parents // row_count
    col_index = (
        reach_ids * (local_outer * row_count)
        + col_source // (row_count * col_count) * row_count
        + col_source % row_count
    )
    col_index = jnp.where(col_present, col_index, 0)
    routed = jnp.take(stacked, col_index, axis=1)
    routed = jnp.where(col_present[None, :, None], routed, jnp.zeros_like(routed))
    routed = routed.reshape(local_outer, col_count, tile_size, cols_local)
    half_outer = local_outer // 2
    leaf_side = lax.axis_index("leaf") % 2
    kept_rows = lax.dynamic_slice_in_dim(routed, leaf_side * half_outer, half_outer, 0)
    sent_rows = lax.dynamic_slice_in_dim(routed, (1 - leaf_side) * half_outer, half_outer, 0)
    partner_rows = swapped(sent_rows, "leaf", 0)
    merged = kept_rows.astype(jnp.float32) + partner_rows.astype(jnp.float32)
    merged = merged.reshape(
        1, half_outer, col_count, 1, tile_size, local_outer, 1, row_count, tile_size
    )
    return (factor_out, merged)


def solution(mesh):
    return jax.shard_map(
        shards,
        mesh=mesh,
        in_specs=(
            P("leaf", None, None, "row", None, None, "col", None, None),
            P("leaf", None, "col", "row", None),
            P("leaf", None),
        ),
        out_specs=(
            P("leaf", None, None, "row", None, "col"),
            P("leaf", None, None, "row", None, None, "col", None, None),
        ),
        check_vma=False,
    )
```

profile of v0, /device:TPU:95, one launch (start us, length us, event | category | flops | bytes accessed | tf_op | source)
XLA Modules:
  0.0 464.1 jit_solution(14215898574408632647)
XLA Ops:
  7.2 5.2 %fusion.1 = f32[2,16,128,1,2,128]{5,4,3,2,1,0:T(2,128)S(1)} fusion(pred[2]{0:T(512)(128)(4,1)S(1)} %get-tuple-element.36, pred[]{:T(512)S(6)} %eq.81, pred[16]{0:T(512)(128)(4,1)S(1)} %iota_compare_fusion.4, pred[2]{0:T(512)(128)(4,1)S(1)} %get-tuple-element.37, bf16[2,16,128,2,2,128]{5,4,3,2,1,0:T(2,128)(2,1)} %bitcast.133, f32[2,128]{1,0:T(2,128)} %bitcast.141), kind=kLoop, calls=%fused_computation.15 | loop fusion | flops 8388608 | bytes 6292501 | tf_op jit(solution)/shard_map/jit(_where)/select_n | solution.py:10
  12.5 2.3 copy.46
  14.7 5.6 %copy.37 = f32[4096,256]{0,1:T(8,128)} copy(f32[4096,256]{1,0:T(8,128)} %bitcast.132) | data formatting | bytes 8388608 | tf_op jit(solution)/shard_map/jit(_where)/select_n | solution.py:10
  20.5 7.6 %reshape.548 = f32[4096,512]{1,0:T(8,128)} reshape(bf16[1,2,16,1,128,2,1,2,128]{8,7,6,5,4,3,2,1,0:T(2,128)(2,1)} %param.3) | data formatting | bytes 12582912 | tf_op jit(solution)/shard_map/convert_element_type | solution.py:40
  28.1 106.0 %all-reduce.3.cloned.1.call-done = f32[4096,256]{0,1:T(8,128)} async-done(((f32[4096,256]{0,1:T(8,128)}), f32[4096,256]{0,1:T(8,128)}) %all-reduce.3.cloned.1.call-update) | async-done | bytes 4194320 | tf_op jit(solution)/shard_map/psum | solution.py:11
  134.2 0.9 slice.75
  135.1 2.3 all_gather.9
  137.6 11.7 %cholesky.50 = f32[128,128]{1,0:T(8,128)S(1)} custom-call(f32[128,128]{1,0:T(8,128)S(1)} %cholesky.118), custom_call_target="Cholesky" | custom-call | tf_op jit(solution)/shard_map/jit(cholesky)/cholesky | solution.py:63
  149.3 0.6 compare_reduce_fusion.3
  150.0 9.8 %custom-call.15 = f32[1,128,128]{1,2,0:T(8,128)S(1)} custom-call(f32[1,128,128]{2,1,0:T(8,128)S(1)} %get-tuple-element.33), custom_call_target="InvertDiagBlocksLowerTriangular" | custom-call | tf_op jit(solution)/shard_map/jit(cholesky)/cholesky | solution.py:63
  160.3 11.7 %cholesky.105 = f32[128,128]{1,0:T(8,128)S(1)} custom-call(f32[128,128]{1,0:T(8,128)S(1)} %convolution_subtract_fusion.1), custom_call_target="Cholesky" | custom-call | tf_op jit(solution)/shard_map/jit(cholesky)/cholesky | solution.py:63
  172.1 0.7 compare_reduce_fusion.2
  174.2 4.0 while.1
  174.4 0.6 fusion.38
  174.9 1.3 bitcast_dynamic-update-slice_fusion.2
  176.3 0.6 fusion.38
  176.9 1.3 bitcast_dynamic-update-slice_fusion.2
  178.3 19.7 %custom-call.16 = f32[2,128,128]{1,2,0:T(8,128)S(1)} custom-call(f32[2,128,128]{2,1,0:T(8,128)S(1)} %get-tuple-element.9), custom_call_target="InvertDiagBlocksLowerTriangular" | custom-call | tf_op jit(solution)/shard_map/jit(_solve_triangular)/triangular_solve | solution.py:64
  197.9 2.4 slice_bitcast_fusion
  200.4 1.9 fusion.3
  202.2 1.9 convolution_subtract_fusion
  204.1 1.9 fusion.10
  206.3 0.5 fusion.2
  206.8 1.4 copy-done
  208.2 0.8 copy.43
  208.9 0.3 constant_dynamic-slice_fusion.2
  209.3 2.2 all_gather.10
  211.7 19.8 %subtract_convert_fusion = bf16[4096,512]{1,0:T(8,128)(2,1)} fusion(f32[4096,512]{1,0:T(8,128)} %reshape.548, f32[512,256]{1,0:T(8,128)S(1)} %bitcast.137, f32[4096]{0:T(1024)S(1)} %bitcast.138, s32[512]{0:T(512)S(1)} %bitcast.144, s32[512]{0:T(512)S(1)} %bitcast.145, s32[4096]{0:T(1024)S(1)} %bitcast.139, s32[4096]{0:T(1024)S(1)} %bitcast.140, ...), kind=kOutput, calls=%fused_computation.5 | convolution fusion | flops 6462373888 | bytes 17359360 | tf_op jit(solution)/shard_map/ik,jk->ij/dot_general | solution.py:81
  231.7 0.5 copy-done.4
  232.6 26.1 %all-gather.3.cloned.1.call-done = bf16[8192,512]{1,0:T(8,128)(2,1)} async-done(((bf16[4096,512]{1,0:T(8,128)(2,1)}), bf16[8192,512]{1,0:T(8,128)(2,1)}) %all-gather.3.cloned.1.call-update) | async-done | bytes 8388624 | tf_op jit(solution)/shard_map/all_gather | solution.py:97
  258.8 6.2 %gather_fusion = bf16[32,128,512]{2,1,0:T(8,128)(2,1)} fusion(bf16[64,128,512]{2,1,0:T(8,128)(2,1)} %bitcast.135, s32[1024]{0:T(1024)S(1)} %pad_clamp_fusion.1), kind=kCustom, calls=%fused_computation | custom fusion | bytes 8388736 | tf_op jit(solution)/shard_map/jit(_take)/gather | solution.py:112
  265.0 6.9 %reshape.568 = bf16[4096,4,128]{2,1,0:T(4,128)(2,1)} reshape(bf16[32,128,512]{2,1,0:T(8,128)(2,1)} %gather_fusion) | data formatting | bytes 8388608 | tf_op jit(solution)/shard_map/jit(_take)/gather | solution.py:112
  271.9 7.4 %copy.38 = bf16[4096,4,128]{0,2,1:T(8,128)(2,1)} copy(bf16[4096,4,128]{2,1,0:T(4,128)(2,1)} %reshape.568) | data formatting | bytes 8388608 | tf_op jit(solution)/shard_map/jit(_take)/gather | solution.py:112
  279.3 4.8 %select_select_fusion.1 = bf16[4096,4,128]{0,2,1:T(8,128)(2,1)} fusion(bf16[4096,4,128]{0,2,1:T(8,128)(2,1)} %copy.38, pred[4096]{0:T(1024)(128)(4,1)S(1)} %get-tuple-element.38, pred[4096]{0:T(1024)(128)(4,1)S(1)} %get-tuple-element.39), kind=kLoop, calls=%fused_computation.14 | loop fusion | flops 4194304 | bytes 8396800 | tf_op jit(solution)/shard_map/jit(_where)/select_n | solution.py:113
  284.1 0.6 collective-permute-start
  285.4 94.3 %collective-permute-done = bf16[4096,4,128]{0,2,1:T(8,128)(2,1)} collective-permute-done((bf16[4096,4,128]{0,2,1:T(8,128)(2,1)}, bf16[4096,4,128]{0,2,1:T(8,128)(2,1)}, u32[]{:S(2)}, u32[]{:S(2)}) %collective-permute-start) | collective-permute-done | bytes 4194336 | tf_op jit(solution)/shard_map/ppermute | solution.py:16
  379.7 7.4 %pad_maximum_fusion = bf16[4096,8,128]{0,2,1:T(8,128)(2,1)} fusion(bf16[4096,4,128]{0,2,1:T(8,128)(2,1)} %collective-permute-done, bf16[4096,4,128]{0,2,1:T(8,128)(2,1)} %select_select_fusion.1), kind=kLoop, calls=%fused_computation.4 | loop fusion | flops 4194304 | bytes 16777216 | tf_op jit(solution)/shard_map/concatenate | solution.py:117
  387.1 6.2 %gather_fusion.1 = bf16[4,4096,128]{1,2,0:T(8,128)(2,1)} fusion(bf16[4096,8,128]{0,2,1:T(8,128)(2,1)} %pad_maximum_fusion, s32[1024]{0:T(1024)S(1)} %pad_clamp_fusion), kind=kCustom, calls=%fused_computation.1 | custom fusion | bytes 8388624 | tf_op jit(solution)/shard_map/jit(_take)/gather | solution.py:130
  393.3 3.4 copy.44
  396.8 2.7 select_select_fusion
  399.5 2.0 copy-done.1
  401.5 0.4 constant_dynamic-slice_fusion.1
  401.8 1.4 collective-permute-start.1
  403.2 1.1 fusion.8
  404.4 0.9 copy.36
  405.2 42.9 %collective-permute-done.1 = bf16[1,16,128,512]{2,1,0,3:T(8,128)(2,1)} collective-permute-done((bf16[1,16,128,512]{2,1,0,3:T(8,128)(2,1)S(1)}, bf16[1,16,128,512]{2,1,0,3:T(8,128)(2,1)}, u32[]{:S(2)}, u32[]{:S(2)}) %collective-permute-start.1) | collective-permute-done | bytes 2097184 | tf_op jit(solution)/shard_map/ppermute | solution.py:22
  448.1 3.9 convert_add_fusion
  452.1 5.2 %copy.39 = f32[1,1,16,1,128,2,1,2,128]{8,7,6,5,4,3,2,1,0:T(2,128)} copy(f32[1,1,16,1,128,2,1,2,128]{4,2,8,7,5,6,3,1,0:T(8,128)} %bitcast.129) | data formatting | bytes 8388608 | tf_op jit(solution)/shard_map/reshape | solution.py:139
  (60 shorter events, 3.2 us)
Async XLA Ops:
  7.2 127.0 %all-reduce.3.cloned.1.call-start = ((), (), s32[]{:S(2)}) async-start(), calls=%async_computation | async-start | bytes 8388608 | tf_op jit(solution)/shard_map/psum | solution.py:11
  20.4 238.3 %all-gather.3.cloned.1.call-start = ((), (), s32[]{:S(2)}) async-start(), calls=%async_computation.1 | async-start | bytes 12582912 | tf_op jit(solution)/shard_map/all_gather | solution.py:97
  206.2 1.9 copy-start
  208.2 3.5 copy-start.3
  231.5 0.7 copy-start.4
  284.1 95.6 %collective-permute-start = (bf16[4096,4,128]{0,2,1:T(8,128)(2,1)}, bf16[4096,4,128]{0,2,1:T(8,128)(2,1)}, u32[]{:S(2)}, u32[]{:S(2)}) collective-permute-start(bf16[4096,4,128]{0,2,1:T(8,128)(2,1)} %select_select_fusion.1), channel_id=1, source_target_pairs={{0,15},{1,0},{2,1},{3,2},{4,3},{5,4},{6,5},{7,6},{8,7},{9,8},{10,9... | collective-permute-start | bytes 12582920 | tf_op jit(solution)/shard_map/ppermute | solution.py:16
  399.5 2.0 copy-start.1
  401.8 46.3 %collective-permute-start.1 = (bf16[1,16,128,512]{2,1,0,3:T(8,128)(2,1)S(1)}, bf16[1,16,128,512]{2,1,0,3:T(8,128)(2,1)}, u32[]{:S(2)}, u32[]{:S(2)}) collective-permute-start(bf16[1,16,128,512]{2,1,0,3:T(8,128)(2,1)S(1)} %constant_dynamic-slice_fusion.1), channel_id=1, source_target_pairs={{0,32},{32,0},{64,96},{96,64},{128,160},{160,128},{192,224},{224,1... | collective-permute-start | bytes 6291464 | tf_op jit(solution)/shard_map/ppermute | solution.py:22
  403.2 44.9 %copy-start.2 = (bf16[2,16,128,512]{2,1,0,3:T(8,128)(2,1)S(1)}, bf16[2,16,128,512]{2,1,0,3:T(8,128)(2,1)}, u32[]{:S(2)}) copy-start(bf16[2,16,128,512]{2,1,0,3:T(8,128)(2,1)} %copy-done.1) | copy-start | bytes 12582916
Sparse Core Ops, SparseCore 0:
  20.5 113.5 all-reduce.2
  231.6 27.0 all-gather.2
where the time goes:
time: 467 us; the launch traced here: 464 us
  waiting for transfers between devices  269 us (58%)
  other arithmetic  81.3 us (17%)
  local copies, waits for them, and re-layouts  65.4 us (14%)
  matrix products  25.9 us (6%)
  between operations  15.6 us (3%)
    psum x1, waiting for transfers between devices, broadcast(): return lax.psum(block, axis)  106 us
    ppermute x1, waiting for transfers between devices, passed_along(): lax.ppermute(array, axis, [(i, (i + by) % length) for i in range(length)])  94.3 us
    ppermute x1, waiting for transfers between devices, swapped(): return lax.ppermute(value, axis, pairs)  42.9 us
    another operation x7, other arithmetic, shards(): factor = jnp.linalg.cholesky(corner)  34.6 us
    all_gather x1, waiting for transfers between devices, shards(): every_rows = lax.all_gather(low_block, 'row', axis=0, tiled=True)  26.1 us
    gather x3, local copies, waits for them, and re-layouts, shards(): routed_rows = jnp.take(every_rows, row_index, axis=0)  20.6 us
    dot_general x1, matrix products, shards(): jnp.einsum('ik,jk->ij', all_panels, all_cols, precision=highest)  19.8 us
    another operation x3, other arithmetic, shards(): jax.scipy.linalg.solve_triangular(factor, slab_cols[tile_size:].T, lower=...  19.7 us
  transfers between devices with their start and end apart: 4, of which 4 were waited for; matrix products, arithmetic and copies ran while one was open for 2% of the time, Pallas kernels for 0%

commit v1 on v0

v1 whole, which is shorter than its diff:
```python
import jax
import jax.numpy as jnp
from jax import lax
from jax.experimental import pallas as pl
from jax.experimental.pallas import tpu as pltpu
from jax.sharding import PartitionSpec as P

T = 128
N = 256
COLS = 16
HALF = 16
CHUNK = 4 * T
PACK = CHUNK + 16
HIGHEST = lax.Precision.HIGHEST
F32 = jnp.float32
BF16 = jnp.bfloat16


def dot(a, b, dims, precision=None):
    return lax.dot_general(a, b, (dims, ((), ())), precision=precision, preferred_element_type=F32)


NN = ((1,), (0,))
NT = ((1,), (1,))
TN = ((0,), (0,))


def strip_factor(strip, start):
    lane = lax.broadcasted_iota(jnp.int32, (8, T), 1)
    sub = lax.broadcasted_iota(jnp.int32, (8, T), 0)
    turned = pltpu.roll(strip[:, :T], lax.rem(T - start, T), axis=1)
    a = {}
    for j in range(8):
        column = jnp.broadcast_to(turned[:, j : j + 1], (8, T))
        for i in range(j, 8):
            a[i, j] = jnp.broadcast_to(column[i : i + 1, :], (8, T))
    low, inv = {}, {}
    for k in range(8):
        inv[k, k] = lax.rsqrt(a[k, k])
        for i in range(k + 1, 8):
            low[i, k] = a[i, k] * inv[k, k]
        for j in range(k + 1, 8):
            for i in range(j, 8):
                a[i, j] = a[i, j] - low[i, k] * low[j, k]
    for k in range(8):
        for i in range(k + 1, 8):
            total = low[i, k] * inv[k, k]
            for m in range(k + 1, i):
                total = total + low[i, m] * inv[m, k]
            inv[i, k] = -inv[i, i] * total
    out = None
    for m in range(8):
        weight = jnp.zeros((8, T), F32)
        for k in range(m, 8):
            weight = jnp.where(sub == k, inv[k, m], weight)
        row = jnp.broadcast_to(strip[m : m + 1, :], (8, 2 * T))
        term = jnp.concatenate([weight, weight], axis=1) * row
        out = term if out is None else out + term
    upper = jnp.where(lane >= start + sub, out[:, :T], 0.0)
    later = jnp.where(lane >= start + 8, out[:, :T], 0.0)
    return jnp.concatenate([upper, out[:, T:]], axis=1), later


def eliminate(work):
    def body(b, carry):
        start = pl.multiple_of(b * 8, 8)
        for l in range(2):
            strip, later = strip_factor(work[l, pl.ds(start, 8), :], start)
            update = dot(later, strip, TN, HIGHEST)
            work[l] = work[l] - update
            work[l, pl.ds(start, 8), :] = strip
        return carry

    lax.fori_loop(0, T // 8, body, 0)


def factor_kernel(s_ref, upper_ref, linv_ref, sinv_ref, work, full):
    eye = jnp.where(
        lax.broadcasted_iota(jnp.int32, (T, T), 0) == lax.broadcasted_iota(jnp.int32, (T, T), 1), 1.0, 0.0
    ).astype(F32)
    for l in range(2):
        work[l, :, :T] = s_ref[l, :T, :T]
        work[l, :, T:] = eye
    eliminate(work)
    for l in range(2):
        inverse = work[l, :, T:]
        across = dot(inverse, s_ref[l, :T, T:], NN, HIGHEST)
        if l == 0:
            upper_ref[:T, :T] = work[l, :, :T]
            upper_ref[:T, T:] = across
            upper_ref[T:, :T] = jnp.zeros((T, T), F32)
        full[l, :T, :T] = inverse
        full[l, :T, T:] = jnp.zeros((T, T), F32)
        full[l, T:, :T] = dot(across, inverse, TN, HIGHEST)
        work[l, :, :T] = s_ref[l, T:, T:] - dot(across, across, TN, HIGHEST)
        work[l, :, T:] = eye
    eliminate(work)
    for l in range(2):
        inverse = work[l, :, T:]
        if l == 0:
            upper_ref[T:, T:] = work[l, :, :T]
        full[l, T:, :T] = -dot(inverse, full[l, T:, :T], NN, HIGHEST)
        full[l, T:, T:] = inverse
        whole = full[l]
        square = dot(whole, whole, TN, HIGHEST)
        high = square.astype(BF16)
        sinv_ref[l, 0] = high
        sinv_ref[l, 1] = (square - high.astype(F32)).astype(BF16)
    whole = full[0]
    high = whole.astype(BF16)
    linv_ref[0] = high
    linv_ref[1] = (whole - high.astype(F32)).astype(BF16)


def factor(top):
    return pl.pallas_call(
        factor_kernel,
        name="factor",
        out_shape=(
            jax.ShapeDtypeStruct((N, N), F32),
            jax.ShapeDtypeStruct((2, N, N), BF16),
            jax.ShapeDtypeStruct((2, 2, N, N), BF16),
        ),
        scratch_shapes=[pltpu.VMEM((2, T, 2 * T), F32), pltpu.VMEM((2, N, N), F32)],
        compiler_params=pltpu.CompilerParams(vmem_limit_bytes=24 << 20),
        cost_estimate=pl.CostEstimate(flops=4 * N**3, bytes_accessed=4 << 20, transcendentals=0),
    )(top)


def place_of(q):
    return (q // 2) % COLS, (q // (2 * COLS)) * 2 + q % 2


def cols_kernel(src, at, p_ref, sinv_ref, out_ref):
    rows = jnp.concatenate([p_ref[0, 0, 0], p_ref[1, 0, 0]], axis=1)
    value = dot(sinv_ref[0, 0], rows, NT) + dot(sinv_ref[0, 1], rows, NT)
    high = value.astype(BF16)
    out_ref[0, 0] = high
    out_ref[0, 1] = (value - high.astype(F32)).astype(BF16)


def cols_factor(src, at, gathered, sinv):
    def p_map(l, j, src, at):
        parent = ((j // 2) * COLS + at[1]) * 2 + j % 2
        chip, slot = place_of(src[l * 64 + parent])
        return (0, chip, l, slot, 0)

    return pl.pallas_call(
        cols_kernel,
        name="cols_factor",
        out_shape=jax.ShapeDtypeStruct((2, 2, N, CHUNK), BF16),
        grid_spec=pltpu.PrefetchScalarGridSpec(
            num_scalar_prefetch=2,
            grid=(2, 4),
            in_specs=[
                pl.BlockSpec((2, 1, 1, T, T), p_map),
                pl.BlockSpec((1, 2, N, N), lambda l, j, src, at: (l, 0, 0, 0)),
            ],
            out_specs=pl.BlockSpec((1, 2, N, T), lambda l, j, src, at: (l, 0, 0, j)),
        ),
        cost_estimate=pl.CostEstimate(flops=8 * 4 * N * N * T, bytes_accessed=4 << 20, transcendentals=0),
    )(src, at, gathered, sinv)


def panel_kernel(at, p_ref, linv_ref, upper_ref, out_ref):
    step = pl.program_id(0)
    row, col = at[0], at[1]
    start = pl.multiple_of(col * 16, 16)
    weights = jnp.concatenate([linv_ref[0, pl.ds(start, 16), :], linv_ref[1, pl.ds(start, 16), :]], axis=0)
    for o in range(2):
        offset = pl.multiple_of((o * 2 + row) * T, T)
        rows = jnp.concatenate([p_ref[0, 0, 0, pl.ds(offset, T), :], p_ref[1, 0, 0, pl.ds(offset, T), :]], axis=1)
        both = dot(weights, rows, NT)
        value = both[:16] + both[16:]
        if o == 0:
            first = upper_ref[pl.ds(start, 16), :T]
            second = upper_ref[pl.ds(start, 16), T:]
            value = jnp.where(step == 0, jnp.where(row == 0, first, second), value)
        out_ref[o, 0] = value


def panel_out(at, gathered, linv, upper):
    return pl.pallas_call(
        panel_kernel,
        name="panel_out",
        out_shape=jax.ShapeDtypeStruct((2, COLS, 16, T), F32),
        grid_spec=pltpu.PrefetchScalarGridSpec(
            num_scalar_prefetch=1,
            grid=(COLS,),
            in_specs=[
                pl.BlockSpec((2, 1, 1, CHUNK, T), lambda i, at: (0, i, 0, 0, 0)),
                pl.BlockSpec((2, N, N), lambda i, at: (0, 0, 0)),
                pl.BlockSpec((N, N), lambda i, at: (0, 0)),
            ],
            out_specs=pl.BlockSpec((2, 1, 16, T), lambda i, at: (0, i, 0, 0)),
        ),
        cost_estimate=pl.CostEstimate(flops=4 * 8192 * N * 16, bytes_accessed=6 << 20, transcendentals=0),
    )(at, gathered, linv, upper)


def parent_kernel(src, at, *refs):
    data, (p_own, p_other, w_ref, reg_ref, out_ref, buf) = refs[:8], refs[8:]
    row, col, base, half = at[0], at[1], at[2], at[3]
    parent_row = 2 * (HALF * half + pl.program_id(0)) + row
    diagonal = lax.broadcasted_iota(jnp.int32, (T, T), 0) == lax.broadcasted_iota(jnp.int32, (T, T), 1)
    for l in range(2):
        from_row = src[l * 64 + parent_row]
        mine = from_row % 2 == row

        @pl.when(mine)
        def _():
            buf[:CHUNK] = data[4 * l][0].astype(F32)
            buf[CHUNK:] = data[4 * l + 1][0].astype(F32)

        @pl.when(jnp.logical_not(mine))
        def _():
            buf[:CHUNK] = data[4 * l + 2][0].astype(F32)
            buf[CHUNK:] = data[4 * l + 3][0].astype(F32)

        p_ref = (p_own, p_other)[l]
        rows = jnp.concatenate([p_ref[0, 0, 0], p_ref[1, 0, 0]], axis=1)
        update = dot(rows, w_ref[l, 0], NN) + dot(rows, w_ref[l, 1], NN)
        for j in range(4):
            parent_col = ((j // 2) * COLS + col) * 2 + j % 2
            from_col = src[l * 64 + parent_col]
            chip, slot = place_of(from_col)
            offset = jnp.where(chip == col, 0, CHUNK) + slot
            value = buf[pl.ds(offset, T, stride=4), :]
            gain = jnp.where(from_row == from_col, 1.0, 0.0) * reg_ref[l, pl.ds(from_col, 1), :]
            value = value + jnp.where(diagonal, gain, 0.0)
            value = value - update[:, j * T : (j + 1) * T]
            value = value.astype(BF16).astype(F32)
            there = jnp.logical_and(from_row > 0, from_col > 0)
            value = jnp.where(there, value, 0.0)
            target = (0, pl.ds(j, T, stride=4), slice(None))
            if l == 0:
                out_ref[target] = value
            else:
                out_ref[target] = out_ref[target] + value


def parent_out(src, at, data, gathered, weights, reg):
    def chunk_spec(l, partner):
        def index(i, src, at):
            q = src[l * 64 + 2 * (HALF * at[3] + i) + at[0]]
            wanted = (q % 2 == at[0]) != partner
            return (jnp.where(wanted, jnp.maximum(q // 2 - at[2], 0), 0), 0, 0)

        return pl.BlockSpec((1, CHUNK, T), index)

    def p_spec(l):
        def index(i, src, at):
            chip, slot = place_of(src[l * 64 + 2 * (HALF * at[3] + i) + at[0]])
            return (0, chip, l, slot, 0)

        return pl.BlockSpec((2, 1, 1, T, T), index)

    return pl.pallas_call(
        parent_kernel,
        name="parent_out",
        out_shape=jax.ShapeDtypeStruct((HALF, CHUNK, T), F32),
        grid_spec=pltpu.PrefetchScalarGridSpec(
            num_scalar_prefetch=2,
            grid=(HALF,),
            in_specs=[chunk_spec(l, p) for l in range(2) for p in (False, True) for _ in range(2)]
            + [
                p_spec(0),
                p_spec(1),
                pl.BlockSpec((2, 2, N, CHUNK), lambda i, src, at: (0, 0, 0, 0)),
                pl.BlockSpec((2, 64, T), lambda i, src, at: (0, 0, 0)),
            ],
            out_specs=pl.BlockSpec((1, CHUNK, T), lambda i, src, at: (i, 0, 0)),
            scratch_shapes=[pltpu.VMEM((2 * CHUNK, T), F32)],
        ),
        compiler_params=pltpu.CompilerParams(vmem_limit_bytes=32 << 20),
        cost_estimate=pl.CostEstimate(flops=2 * 2 * 4096 * N * CHUNK, bytes_accessed=14 << 20, transcendentals=0),
    )(src, at, *data, gathered, gathered, weights, reg)


def turned(value, axis, length, by):
    return lax.ppermute(value, axis, [(i, (i + by) % length) for i in range(length)])


def swapped(value, axis, length):
    return lax.ppermute(value, axis, [(i, i ^ 1) for i in range(length)])


def shards(front_tiles, regular, child_map):
    leaves = lax.axis_size("leaf")
    row, col = lax.axis_index("row"), lax.axis_index("col")
    half = lax.axis_index("leaf") % 2
    base = jnp.where(half == 0, 1, HALF)
    tiles = front_tiles.reshape(2 * COLS, CHUNK, T)

    columns = tiles[0].reshape(T, 4, T).transpose(1, 2, 0).reshape(CHUNK, T)
    gains = regular.reshape(2, T)
    high = lax.reduce_precision(gains, 8, 7)
    rest = gains - high
    middle = lax.reduce_precision(rest, 8, 7)
    pieces = jnp.concatenate([high, middle, rest - middle], axis=0).astype(BF16)
    parents = jnp.arange(64, dtype=jnp.int32)
    match = child_map.reshape(1, -1) == parents[:, None]
    source = jnp.sum(jnp.where(match, 2 + jnp.arange(62, dtype=jnp.int32)[None, :], 0), axis=1)
    source = jnp.pad(source, (0, T - 64)).astype(BF16)[None]
    pack = jnp.concatenate([columns, pieces, source, jnp.zeros((9, T), BF16)], axis=0)
    packs = jnp.stack([pack, swapped(pack, "leaf", leaves)])
    gathered = lax.all_gather(packs, ("row", "col"), axis=0, tiled=False)
    gathered = gathered.reshape(2, COLS, 2, PACK, T)

    keep = lax.dynamic_slice_in_dim(tiles, base, HALF, 0)
    send = lax.dynamic_slice_in_dim(tiles, HALF + 1 - base, HALF, 0)
    other = swapped(send, "leaf", leaves)
    keep_next = turned(keep, "col", COLS, -1)
    other_next = turned(other, "col", COLS, -1)
    data = [keep, keep_next, swapped(keep, "row", 2), swapped(keep_next, "row", 2)]
    data += [other, other_next, swapped(other, "row", 2), swapped(other_next, "row", 2)]

    pieces = gathered[:, :, :, CHUNK : CHUNK + 6].astype(F32).reshape(2, COLS, 2, 3, 2, T)
    reg = (pieces[:, :, :, 0] + pieces[:, :, :, 1]) + pieces[:, :, :, 2]
    reg = reg.transpose(2, 3, 1, 0, 4).reshape(2, 64, T)
    src = gathered[0, 0, :, CHUNK + 6, :64].astype(jnp.int32).reshape(-1)
    top = gathered[:, 0, :, :N].transpose(1, 2, 0, 3).reshape(2, N, N).astype(F32)
    top = top + jnp.where(jnp.eye(N, dtype=jnp.bool_)[None], reg[:, :2].reshape(2, 1, N), 0.0)
    at = jnp.stack([row, col, base, half]).astype(jnp.int32)

    upper, linv, sinv = factor(top)
    weights = cols_factor(src, at, gathered, sinv)
    panel = panel_out(at, gathered, linv, upper)
    panel = panel.transpose(0, 1, 3, 2).reshape(1, 2, COLS, 1, T, 16)
    parent = parent_out(src, at, data, gathered, weights, reg)
    return panel, parent.reshape(1, 1, COLS, 1, T, 2, 1, 2, T)


def solution(mesh):
    return jax.shard_map(
        shards,
        mesh=mesh,
        in_specs=(
            P("leaf", None, None, "row", None, None, "col", None, None),
            P("leaf", None, "col", "row", None),
            P("leaf", None),
        ),
        out_specs=(
            P("leaf", None, None, "row", None, "col"),
            P("leaf", None, None, "row", None, None, "col", None, None),
        ),
        check_vma=False,
    )
```

time: 467 us -> 251 us (0.54)
  waiting for transfers between devices: 269 us -> 124 us
  Pallas kernels: 0 us -> 80.2 us
  other arithmetic: 81.3 us -> 5.57 us
  local copies, waits for them, and re-layouts: 65.4 us -> 8.4 us
  matrix products: 25.9 us -> 0 us
  starting transfers between devices: 2.01 us -> 14.7 us
    psum x1 -> x0, waiting for transfers between devices: 106 us -> none  [broadcast(): return lax.psum(block, axis)]
    pallas_call x0 -> x4, Pallas kernels: none -> 80.2 us  [the longest x1 43.4 us: factor(): pl.pallas_call(factor_kernel, name='factor', out_shape=(jax.ShapeDtypeStr...]
    another operation x10 -> x4, other arithmetic: 54.3 us -> 2.09 us  [the longest x1 0.73 us: shards(): packs = jnp.stack([pack, swapped(pack, 'leaf', leaves)])]
    ppermute x2 -> x8, waiting for transfers between devices: 137 us -> 92.4 us  [the longest x6 47.3 us: swapped(): return lax.ppermute(value, axis, [(i, i ^ 1) for i in range(length)])]
    gather x4 -> x0, local copies, waits for them, and re-layouts: 26.8 us -> none  [the longest x3 20.6 us: shards(): routed_rows = jnp.take(every_rows, row_index, axis=0)]
    dot_general x1 -> x0, matrix products: 19.8 us -> none  [shards(): jnp.einsum('ik,jk->ij', all_panels, all_cols, precision=highest)]
    ppermute x2 -> x8, starting transfers between devices: 1.93 us -> 14.7 us  [the longest x6 13.6 us: swapped(): return lax.ppermute(value, axis, [(i, i ^ 1) for i in range(length)])]
    select_n x5 -> x0, other arithmetic: 12.7 us -> none  [the longest x1 5.2 us: broadcast(): jnp.where(lax.axis_index(axis) == source, block, jnp.zeros_like(block))]
  transfers between devices with their start and end apart: 4 -> 9, of which waited for: 4 -> 5; matrix products, arithmetic and copies ran while one was open for 2% -> 3% of each run, Pallas kernels for 0% -> 25%
where the time goes in v1:
time: 251 us; the launch traced here: 247 us
  waiting for transfers between devices  124 us (49%)
  Pallas kernels  80.2 us (32%)
  starting transfers between devices  14.7 us (6%)
  between operations  14.2 us (6%)
  local copies, waits for them, and re-layouts  8.4 us (3%)
  other arithmetic  5.57 us (2%)
    ppermute x6, waiting for transfers between devices, swapped(): return lax.ppermute(value, axis, [(i, i ^ 1) for i in range(length)])  47.3 us
    ppermute x2, waiting for transfers between devices, turned(): lax.ppermute(value, axis, [(i, (i + by) % length) for i in range(length)])  45.1 us
    pallas_call x1, Pallas kernels, factor(): pl.pallas_call(factor_kernel, name='factor', out_shape=(jax.ShapeDtypeStr...  43.4 us
    all_gather x1, waiting for transfers between devices, shards(): gathered = lax.all_gather(packs, ('row', 'col'), axis=0, tiled=False)  31.1 us
    pallas_call x1, Pallas kernels, parent_out(): pl.pallas_call(parent_kernel, name='parent_out', out_shape=jax.ShapeDtype...  18.5 us
    ppermute x6, starting transfers between devices, swapped(): return lax.ppermute(value, axis, [(i, i ^ 1) for i in range(length)])  13.6 us
    pallas_call x1, Pallas kernels, panel_out(): pl.pallas_call(panel_kernel, name='panel_out', out_shape=jax.ShapeDtypeSt...  11.2 us
    pallas_call x1, Pallas kernels, cols_factor(): pl.pallas_call(cols_kernel, name='cols_factor', out_shape=jax.ShapeDtypeS...  6.97 us
  transfers between devices with their start and end apart: 9, of which 5 were waited for; matrix products, arithmetic and copies ran while one was open for 3% of the time, Pallas kernels for 25%

profile of v1, /device:TPU:95, one launch (start us, length us, event | category | flops | bytes accessed | tf_op | source)
XLA Modules:
  0.0 246.7 jit_solution(3715418278888457812)
XLA Ops:
  7.2 0.0 all-gather.3.cloned.1.call-start
  7.2 0.8 select_reduce_fusion
  8.0 0.7 fusion.1
  8.7 0.9 slice.32
  9.6 0.1 copy.32
  9.8 0.2 concatenate.6
  10.0 1.7 collective-permute-start
  11.7 3.2 %collective-permute-done = bf16[528,128]{1,0:T(8,128)(2,1)S(1)} collective-permute-done((bf16[528,128]{1,0:T(8,128)(2,1)S(1)}, bf16[528,128]{1,0:T(8,128)(2,1)S(1)}, u32[]{:S(2)}, u32[]{:S(2)}) %collective-permute-start) | collective-permute-done | bytes 135200 | tf_op jit(solution)/shard_map/ppermute | solution.py:285
  14.9 0.7 pad_maximum_fusion
  15.6 0.0 all-gather.3.cloned.1.call-update
  15.6 2.6 %constant_dynamic-slice_fusion = (bf16[16,512,128]{2,1,0:T(8,128)(2,1)S(1)}, bf16[16,512,128]{2,1,0:T(8,128)(2,1)S(1)}) fusion(bf16[32,512,128]{2,1,0:T(8,128)(2,1)} %bitcast.53, s32[]{:T(128)S(6)} %select_n.27, s32[]{:T(128)} %select_n.24), kind=kLoop, calls=%fused_computation.23 | loop fusion | bytes 8388616 | tf_op jit(solution)/shard_map/dynamic_slice | solution.py:311
  18.2 1.3 collective-permute-start.4
  19.6 0.5 collective-permute-start.1
  20.1 44.1 %collective-permute-done.4.refs_4_ = bf16[16,512,128]{2,1,0:T(8,128)(2,1)} collective-permute-done((bf16[16,512,128]{2,1,0:T(8,128)(2,1)S(1)}, bf16[16,512,128]{2,1,0:T(8,128)(2,1)}, u32[]{:S(2)}, u32[]{:S(2)}) %collective-permute-start.4) | collective-permute-done | bytes 2097184 | tf_op jit(solution)/shard_map/ppermute | solution.py:285
  64.2 0.5 collective-permute-start.5
  64.7 2.6 %collective-permute-start.2 = (bf16[16,512,128]{2,1,0:T(8,128)(2,1)S(1)}, bf16[16,512,128]{2,1,0:T(8,128)(2,1)}, u32[]{:S(2)}, u32[]{:S(2)}) collective-permute-start(bf16[16,512,128]{2,1,0:T(8,128)(2,1)S(1)} %get-tuple-element.19.refs_0_), channel_id=1, source_target_pairs={{0,16},{16,0},{1,17},{17,1},{2,18},{18,2},{3,19},{19,3},{4,20},{20... | collective-permute-start | bytes 6291464 | tf_op jit(solution)/shard_map/ppermute | solution.py:285
  67.3 0.0 collective-permute-start.6
  67.3 5.3 %collective-permute-done.1.refs_1_ = bf16[16,512,128]{2,1,0:T(8,128)(2,1)} collective-permute-done((bf16[16,512,128]{2,1,0:T(8,128)(2,1)S(1)}, bf16[16,512,128]{2,1,0:T(8,128)(2,1)}, u32[]{:S(2)}, u32[]{:S(2)}) %collective-permute-start.1) | collective-permute-done | bytes 2097184 | tf_op jit(solution)/shard_map/ppermute | solution.py:281
  72.6 5.2 %collective-permute-start.3 = (bf16[16,512,128]{2,1,0:T(8,128)(2,1)}, bf16[16,512,128]{2,1,0:T(8,128)(2,1)}, u32[]{:S(2)}, u32[]{:S(2)}) collective-permute-start(bf16[16,512,128]{2,1,0:T(8,128)(2,1)} %collective-permute-done.1.refs_1_), channel_id=1, source_target_pairs={{0,16},{16,0},{1,17},{17,1},{2,18},{18,2},{3,19},{19,3},{4,20},{20... | collective-permute-start | bytes 6291464 | tf_op jit(solution)/shard_map/ppermute | solution.py:285
  77.8 39.8 %collective-permute-done.5.refs_5_ = bf16[16,512,128]{2,1,0:T(8,128)(2,1)} collective-permute-done((bf16[16,512,128]{2,1,0:T(8,128)(2,1)}, bf16[16,512,128]{2,1,0:T(8,128)(2,1)}, u32[]{:S(2)}, u32[]{:S(2)}) %collective-permute-start.5) | collective-permute-done | bytes 2097184 | tf_op jit(solution)/shard_map/ppermute | solution.py:281
  117.6 2.8 %collective-permute-start.7 = (bf16[16,512,128]{2,1,0:T(8,128)(2,1)}, bf16[16,512,128]{2,1,0:T(8,128)(2,1)}, u32[]{:S(2)}, u32[]{:S(2)}) collective-permute-start(bf16[16,512,128]{2,1,0:T(8,128)(2,1)} %collective-permute-done.5.refs_5_), channel_id=1, source_target_pairs={{0,16},{16,0},{1,17},{17,1},{2,18},{18,2},{3,19},{19,3},{4,20},{20... | collective-permute-start | bytes 6291464 | tf_op jit(solution)/shard_map/ppermute | solution.py:285
  120.4 0.7 pad_add_fusion.at
  121.1 31.1 %all-gather.3.cloned.1.call-done = bf16[64,528,128]{2,1,0:T(8,128)(2,1)} async-done(((bf16[2,528,128]{2,1,0:T(8,128)(2,1)}), bf16[64,528,128]{2,1,0:T(8,128)(2,1)}) %all-gather.3.cloned.1.call-update) | async-done | bytes 8650768 | tf_op jit(solution)/shard_map/all_gather | solution.py:307
  152.2 0.7 fusion.2
  152.9 0.6 reshape.68.src
  153.6 0.9 slice_convert_fusion
  154.5 0.1 copy.34
  154.6 0.1 copy.35
  154.7 1.0 convert_bitcast_fusion
  155.7 0.2 copy.33
  155.9 0.2 copy.36
  156.1 0.1 select_add_fusion.s_ref
  156.1 43.4 %factor.1 = (f32[256,256]{1,0:T(8,128)S(1)}, bf16[2,256,256]{2,1,0:T(8,128)(2,1)S(1)}, bf16[2,2,256,256]{3,2,1,0:T(8,128)(2,1)S(1)}) custom-call(f32[2,256,256]{2,1,0:T(8,128)S(1)} %select_add_fusion.s_ref), custom_call_target="tpu_custom_call" | custom-call | flops 67108864 | bytes 4194304 | tf_op jit(solution)/shard_map/factor/pallas_call | solution.py:116
  199.6 0.0 copy-start.1
  199.6 0.8 copy-done.1
  200.4 0.7 copy-done.2
  201.1 0.7 copy-done.3
  201.8 11.2 %panel_out.1 = f32[2,16,16,128]{3,2,1,0:T(8,128)} custom-call(s32[4]{0:T(128)} %pad_add_fusion.at, bf16[2,16,2,528,128]{4,3,2,1,0:T(8,128)(2,1)} %bitcast.48, bf16[2,256,256]{2,1,0:T(8,128)(2,1)} %copy-done.3, f32[256,256]{1,0:T(8,128)} %copy-done.2), custom_call_target="tpu_custom_call" | custom-call | flops 134217728 | bytes 6291456 | tf_op jit(solution)/shard_map/panel_out/pallas_call | solution.py:183
  213.0 7.0 %cols_factor.1.refs_10_ = bf16[2,2,256,512]{3,2,1,0:T(8,128)(2,1)} custom-call(s32[128]{0:T(128)} %reshape.68.src, s32[4]{0:T(128)} %pad_add_fusion.at, bf16[2,16,2,528,128]{4,3,2,1,0:T(8,128)(2,1)} %bitcast.49, bf16[2,2,256,256]{3,2,1,0:T(8,128)(2,1)} %copy-done.1), custom_call_target="tpu_custom_call" | custom-call | flops 268435456 | bytes 4194304 | tf_op jit(solution)/shard_map/cols_factor/pallas_call | solution.py:148
  220.0 0.0 collective-permute-done.2.refs_2_
  220.0 0.0 collective-permute-done.6.refs_6_
  220.0 0.0 collective-permute-done.3.refs_3_
  220.0 0.0 collective-permute-done.7.refs_7_
  220.0 0.0 copy-done.4
  220.0 0.0 copy-done.5
  220.0 0.0 copy-start
  220.1 1.2 copy-done
  221.3 18.5 %parent_out.1 = f32[16,512,128]{2,1,0:T(8,128)} custom-call(s32[128]{0:T(128)S(1)} %copy-done.5, s32[4]{0:T(128)S(1)} %copy-done.4, bf16[16,512,128]{2,1,0:T(8,128)(2,1)S(1)} %get-tuple-element.19.refs_0_, bf16[16,512,128]{2,1,0:T(8,128)(2,1)} %collective-permute-done.1.refs_1_, bf16[16,512,128]{2,1,0:T(8,128)(2,1)} %collective-permute-done.2.refs_2_, ...), custom_call_target="tpu_custom_call" | custom-call | flops 2147483648 | bytes 14680064 | tf_op jit(solution)/shard_map/parent_out/pallas_call | solution.py:258
  (12 shorter events, 0.1 us)
Async XLA Ops:
  7.2 145.1 %all-gather.3.cloned.1.call-start = ((), (), s32[]{:S(2)}) async-start(), calls=%async_computation | async-start | bytes 8921088 | tf_op jit(solution)/shard_map/all_gather | solution.py:307
  10.0 4.9 %collective-permute-start = (bf16[528,128]{1,0:T(8,128)(2,1)S(1)}, bf16[528,128]{1,0:T(8,128)(2,1)S(1)}, u32[]{:S(2)}, u32[]{:S(2)}) collective-permute-start(bf16[528,128]{1,0:T(8,128)(2,1)S(1)} %concatenate.6), channel_id=1, source_target_pairs={{0,32},{32,0},{64,96},{96,64},{128,160},{160,128},{192,224},{224,1... | collective-permute-start | bytes 405512 | tf_op jit(solution)/shard_map/ppermute | solution.py:285
  18.2 46.0 %collective-permute-start.4 = (bf16[16,512,128]{2,1,0:T(8,128)(2,1)S(1)}, bf16[16,512,128]{2,1,0:T(8,128)(2,1)}, u32[]{:S(2)}, u32[]{:S(2)}) collective-permute-start(bf16[16,512,128]{2,1,0:T(8,128)(2,1)S(1)} %get-tuple-element.18), channel_id=1, source_target_pairs={{0,32},{32,0},{64,96},{96,64},{128,160},{160,128},{192,224},{224,1... | collective-permute-start | bytes 6291464 | tf_op jit(solution)/shard_map/ppermute | solution.py:285
  19.6 53.1 %collective-permute-start.1 = (bf16[16,512,128]{2,1,0:T(8,128)(2,1)S(1)}, bf16[16,512,128]{2,1,0:T(8,128)(2,1)}, u32[]{:S(2)}, u32[]{:S(2)}) collective-permute-start(bf16[16,512,128]{2,1,0:T(8,128)(2,1)S(1)} %get-tuple-element.19.refs_0_), channel_id=1, source_target_pairs={{0,15},{1,0},{2,1},{3,2},{4,3},{5,4},{6,5},{7,6},{8,7},{9,8},{10,9... | collective-permute-start | bytes 6291464 | tf_op jit(solution)/shard_map/ppermute | solution.py:281
  64.2 53.4 %collective-permute-start.5 = (bf16[16,512,128]{2,1,0:T(8,128)(2,1)}, bf16[16,512,128]{2,1,0:T(8,128)(2,1)}, u32[]{:S(2)}, u32[]{:S(2)}) collective-permute-start(bf16[16,512,128]{2,1,0:T(8,128)(2,1)} %collective-permute-done.4.refs_4_), channel_id=1, source_target_pairs={{0,15},{1,0},{2,1},{3,2},{4,3},{5,4},{6,5},{7,6},{8,7},{9,8},{10,9... | collective-permute-start | bytes 6291464 | tf_op jit(solution)/shard_map/ppermute | solution.py:281
  64.7 155.3 %collective-permute-start.2 = (bf16[16,512,128]{2,1,0:T(8,128)(2,1)S(1)}, bf16[16,512,128]{2,1,0:T(8,128)(2,1)}, u32[]{:S(2)}, u32[]{:S(2)}) collective-permute-start(bf16[16,512,128]{2,1,0:T(8,128)(2,1)S(1)} %get-tuple-element.19.refs_0_), channel_id=1, source_target_pairs={{0,16},{16,0},{1,17},{17,1},{2,18},{18,2},{3,19},{19,3},{4,20},{20... | collective-permute-start | bytes 6291464 | tf_op jit(solution)/shard_map/ppermute | solution.py:285
  67.3 152.7 %collective-permute-start.6 = (bf16[16,512,128]{2,1,0:T(8,128)(2,1)}, bf16[16,512,128]{2,1,0:T(8,128)(2,1)}, u32[]{:S(2)}, u32[]{:S(2)}) collective-permute-start(bf16[16,512,128]{2,1,0:T(8,128)(2,1)} %collective-permute-done.4.refs_4_), channel_id=1, source_target_pairs={{0,16},{16,0},{1,17},{17,1},{2,18},{18,2},{3,19},{19,3},{4,20},{20... | collective-permute-start | bytes 6291464 | tf_op jit(solution)/shard_map/ppermute | solution.py:285
  72.6 147.4 %collective-permute-start.3 = (bf16[16,512,128]{2,1,0:T(8,128)(2,1)}, bf16[16,512,128]{2,1,0:T(8,128)(2,1)}, u32[]{:S(2)}, u32[]{:S(2)}) collective-permute-start(bf16[16,512,128]{2,1,0:T(8,128)(2,1)} %collective-permute-done.1.refs_1_), channel_id=1, source_target_pairs={{0,16},{16,0},{1,17},{17,1},{2,18},{18,2},{3,19},{19,3},{4,20},{20... | collective-permute-start | bytes 6291464 | tf_op jit(solution)/shard_map/ppermute | solution.py:285
  117.6 102.4 %collective-permute-start.7 = (bf16[16,512,128]{2,1,0:T(8,128)(2,1)}, bf16[16,512,128]{2,1,0:T(8,128)(2,1)}, u32[]{:S(2)}, u32[]{:S(2)}) collective-permute-start(bf16[16,512,128]{2,1,0:T(8,128)(2,1)} %collective-permute-done.5.refs_5_), channel_id=1, source_target_pairs={{0,16},{16,0},{1,17},{17,1},{2,18},{18,2},{3,19},{19,3},{4,20},{20... | collective-permute-start | bytes 6291464 | tf_op jit(solution)/shard_map/ppermute | solution.py:285
  199.6 0.8 copy-start.1
  200.4 0.7 copy-start.2
  201.1 0.7 copy-start.3
  213.0 7.0 %copy-start.4 = (s32[4]{0:T(128)S(1)}, s32[4]{0:T(128)}, u32[]{:S(2)}) copy-start(s32[4]{0:T(128)} %pad_add_fusion.at) | copy-start | bytes 52
  213.0 7.0 %copy-start.5 = (s32[128]{0:T(128)S(1)}, s32[128]{0:T(128)}, u32[]{:S(2)}) copy-start(s32[128]{0:T(128)} %reshape.68.src) | copy-start | bytes 1540
  220.0 1.2 copy-start
Sparse Core Ops, SparseCore 0:
  15.7 136.4 all-gather.2

commit v2 on v1

v2 whole, which is shorter than its diff:
```python
import jax
import jax.numpy as jnp
from jax import lax
from jax.experimental import pallas as pl
from jax.experimental.pallas import tpu as pltpu
from jax.sharding import PartitionSpec as P

T = 128
N = 256
COLS = 16
HALF = 16
CHUNK = 4 * T
PACK = CHUNK + 16
HIGHEST = lax.Precision.HIGHEST
F32 = jnp.float32
BF16 = jnp.bfloat16


def dot(a, b, dims, precision=None):
    return lax.dot_general(a, b, (dims, ((), ())), precision=precision, preferred_element_type=F32)


NN = ((1,), (0,))
NT = ((1,), (1,))
TN = ((0,), (0,))


def strip_factor(strip, start):
    lane = lax.broadcasted_iota(jnp.int32, (8, T), 1)
    sub = lax.broadcasted_iota(jnp.int32, (8, T), 0)
    turned = pltpu.roll(strip[:, :T], lax.rem(T - start, T), axis=1)
    a = {}
    for j in range(8):
        column = jnp.broadcast_to(turned[:, j : j + 1], (8, T))
        for i in range(j, 8):
            a[i, j] = jnp.broadcast_to(column[i : i + 1, :], (8, T))
    low, inv = {}, {}
    for k in range(8):
        inv[k, k] = lax.rsqrt(a[k, k])
        for i in range(k + 1, 8):
            low[i, k] = a[i, k] * inv[k, k]
        for j in range(k + 1, 8):
            for i in range(j, 8):
                a[i, j] = a[i, j] - low[i, k] * low[j, k]
    for k in range(8):
        for i in range(k + 1, 8):
            total = low[i, k] * inv[k, k]
            for m in range(k + 1, i):
                total = total + low[i, m] * inv[m, k]
            inv[i, k] = -inv[i, i] * total
    out = None
    for m in range(8):
        weight = jnp.zeros((8, T), F32)
        for k in range(m, 8):
            weight = jnp.where(sub == k, inv[k, m], weight)
        row = jnp.broadcast_to(strip[m : m + 1, :], (8, 2 * T))
        term = jnp.concatenate([weight, weight], axis=1) * row
        out = term if out is None else out + term
    upper = jnp.where(lane >= start + sub, out[:, :T], 0.0)
    later = jnp.where(lane >= start + 8, out[:, :T], 0.0)
    return jnp.concatenate([upper, out[:, T:]], axis=1), later


def split(value):
    high = value.astype(BF16)
    return high, (value - high.astype(F32)).astype(BF16)


def eliminate(work):
    def body(b, carry):
        start = pl.multiple_of(b * 8, 8)
        for l in range(2):
            strip, later = strip_factor(work[l, pl.ds(start, 8), :], start)
            high, low = split(strip)
            later_high, later_low = split(later)
            left = jnp.concatenate([later_high.astype(F32), later_high.astype(F32), later_low.astype(F32)], axis=0)
            right = jnp.concatenate([high.astype(F32), low.astype(F32), high.astype(F32)], axis=0)
            work[l] = work[l] - dot(left.astype(BF16), right.astype(BF16), TN)
            work[l, pl.ds(start, 8), :] = strip
        return carry

    lax.fori_loop(0, T // 8, body, 0)


def factor(top, work, full, upper, linv, sinv, between):
    eye = lax.broadcasted_iota(jnp.int32, (T, T), 0) == lax.broadcasted_iota(jnp.int32, (T, T), 1)
    one = jnp.where(eye, 1.0, 0.0).astype(F32)

    def block(q, s, l):
        value = top[s, l, q * T : (q + 1) * T, :].astype(F32)
        if q == s:
            parts = top[s, l, CHUNK : CHUNK + 16, :].astype(F32)
            gain = (parts[0:1] + parts[2:3]) + parts[4:5]
            value = value + jnp.where(eye, gain, 0.0)
        return value

    for l in range(2):
        work[l, :, :T] = block(0, 0, l)
        work[l, :, T:] = one
    eliminate(work)
    between()
    for l in range(2):
        inverse = work[l, :, T:]
        across = dot(inverse, block(0, 1, l), NN, HIGHEST)
        if l == 0:
            upper[:, :T] = jnp.concatenate([work[l, :, :T], jnp.zeros((T, T), F32)], axis=0)
            upper[:T, T:] = across
        full[l, :T, :T] = inverse
        full[l, :T, T:] = jnp.zeros((T, T), F32)
        full[l, T:, :T] = dot(across, inverse, TN, HIGHEST)
        work[l, :, :T] = block(1, 1, l) - dot(across, across, TN, HIGHEST)
        work[l, :, T:] = one
    eliminate(work)
    for l in range(2):
        inverse = work[l, :, T:]
        if l == 0:
            upper[T:, T:] = work[l, :, :T]
        full[l, T:, :T] = -dot(inverse, full[l, T:, :T], NN, HIGHEST)
        full[l, T:, T:] = inverse
        whole = full[l]
        sinv[l, 0], sinv[l, 1] = split(dot(whole, whole, TN, HIGHEST))
    linv[0], linv[1] = split(full[0])


PARTS = 4
ROWS = HALF // PARTS
MESH = pl.DeviceIdType.MESH


def exchange_kernel(
    tiles, pack, kn, oth, on, kx, knx, ox, onx, spread, panel, sinv, reg,
    top, own, gains, work, full, upper, linv,
    local_sem, z_sem, x_sem, y_sem, core_sem, bulk_sem, pass_sem,
):
    leaf, row, col = lax.axis_index("leaf"), lax.axis_index("row"), lax.axis_index("col")
    y, x = col // 4, col % 4
    sibling = leaf + 1 - 2 * (leaf % 2)
    before, after = lax.rem(col + COLS - 1, COLS), lax.rem(col + 1, COLS)
    half = leaf % 2
    keep = 1 + half * (HALF - 1)
    send = HALF - half * (HALF - 1)
    here = (leaf, row, col)
    across = (leaf, 1 - row, col)
    x_peer = [(leaf, row, y * 4 + lax.rem(x + d, 4)) for d in (1, 2, 3)]
    y_peer = [(leaf, row, lax.rem(y + d, 4) * 4 + x) for d in (1, 2, 3)]

    peers = [(sibling, row, col), (sibling, row, before), (sibling, row, after)]
    peers += [(leaf, row, before), (leaf, row, after), across] + x_peer + y_peer
    barrier = pltpu.get_barrier_semaphore()
    for peer in peers:
        pl.semaphore_signal(barrier, inc=1, device_id=peer, device_id_type=MESH)
    pl.semaphore_wait(barrier, len(peers))

    def remote(source, target, sems, peer):
        return pltpu.make_async_remote_copy(
            src_ref=source, dst_ref=target, send_sem=sems.at[0], recv_sem=sems.at[1],
            device_id=peer, device_id_type=MESH,
        )

    sent = []

    def start(copy):
        copy.start()
        sent.append(copy)
        return copy

    to_sibling = start(remote(pack, spread.at[row, y, x, 1], z_sem, (sibling, row, col)))
    x_copies = [start(remote(pack, spread.at[row, y, x, 0], x_sem.at[0, d], x_peer[d])) for d in range(3)]
    place = pltpu.make_async_copy(pack, spread.at[row, y, x, 0], local_sem.at[0])
    place.start()
    to_sibling.wait_recv()
    x_copies += [
        start(remote(spread.at[row, y, x, 1], spread.at[row, y, x, 1], x_sem.at[1, d], x_peer[d])) for d in range(3)
    ]

    bulk = []
    for k in range(PARTS):
        kept, gone = tiles.at[pl.ds(keep + k * ROWS, ROWS)], tiles.at[pl.ds(send + k * ROWS, ROWS)]
        part = pl.ds(k * ROWS, ROWS)
        bulk.append([
            start(remote(kept, kn.at[part], bulk_sem.at[0, k], (leaf, row, before))),
            start(remote(gone, oth.at[part], bulk_sem.at[1, k], (sibling, row, col))),
            start(remote(gone, on.at[part], bulk_sem.at[2, k], (sibling, row, before))),
            start(remote(kept, kx.at[part], bulk_sem.at[3, k], across)),
        ])

    place.wait()
    for copy in x_copies:
        copy.wait_recv()
    y_copies = [
        [start(remote(spread.at[row, y, g], spread.at[row, y, g], y_sem.at[g, d], y_peer[d])) for d in range(3)]
        for g in range(4)
    ]

    core_copies = []

    def over_core(g):
        for copy in y_copies[g]:
            copy.wait_recv()
        core_copies.append(start(remote(spread.at[row, :, g], spread.at[row, :, g], core_sem.at[g], across)))

    over_core(0)
    core_copies[0].wait_recv()
    loads = [pltpu.make_async_copy(spread.at[s, 0, 0], top.at[s], local_sem.at[1 + s]) for s in range(2)]
    for load in loads:
        load.start()
    for load in loads:
        load.wait()

    def between():
        over_core(1)
        over_core(2)

    factor(top, work, full, upper, linv, sinv, between)
    over_core(3)
    for copy in core_copies[1:]:
        copy.wait_recv()
    loads = [pltpu.make_async_copy(spread.at[:, :, :, 0, pl.ds(0, CHUNK)], own, local_sem.at[3])]
    loads += [pltpu.make_async_copy(spread.at[:, :, :, :, pl.ds(CHUNK, 16)], gains, local_sem.at[4])]
    for load in loads:
        load.start()
    for load in loads:
        load.wait()

    first = pl.multiple_of(col * 16, 16)
    weights = jnp.concatenate([linv[0, pl.ds(first, 16), :], linv[1, pl.ds(first, 16), :]], axis=0)

    def chip(at, carry):
        ay, ax = at // 4, at % 4
        for o in range(2):
            span = pl.ds(pl.multiple_of((o * 2 + row) * T, T), T)
            rows = jnp.concatenate([own[0, ay, ax, span, :], own[1, ay, ax, span, :]], axis=1)
            both = dot(weights, rows, NT)
            panel[o, at] = both[:16] + both[16:]
        for s in range(2):
            for l in range(2):
                parts = gains[s, ay, ax, l].astype(F32)
                for o in range(2):
                    gain = (parts[o : o + 1] + parts[2 + o : 3 + o]) + parts[4 + o : 5 + o]
                    reg[l, pl.ds((o * COLS + at) * 2 + s, 1), :] = gain
        return carry

    lax.fori_loop(0, COLS, chip, 0)
    panel[0, 0] = upper[pl.ds(first, 16), pl.ds(pl.multiple_of(row * T, T), T)]

    passed = []
    for k in range(PARTS):
        part = pl.ds(k * ROWS, ROWS)
        for n, (source, target) in enumerate(((kn, knx), (oth, ox), (on, onx))):
            bulk[k][n].wait_recv()
            passed.append(start(remote(source.at[part], target.at[part], pass_sem.at[n, k], across)))
    for k in range(PARTS):
        bulk[k][3].wait_recv()
    for copy in passed:
        copy.wait_recv()
    for copy in sent:
        copy.wait_send()


def exchange(tiles, pack):
    big = jax.ShapeDtypeStruct((HALF, CHUNK, T), BF16)
    spread = jax.ShapeDtypeStruct((2, 4, 4, 2, PACK, T), BF16)
    dma = pltpu.SemaphoreType.DMA
    anywhere, vmem = pl.BlockSpec(memory_space=pl.ANY), pl.BlockSpec(memory_space=pltpu.VMEM)
    return pl.pallas_call(
        exchange_kernel,
        name="exchange",
        out_shape=(big,) * 7 + (
            spread,
            jax.ShapeDtypeStruct((2, COLS, 16, T), F32),
            jax.ShapeDtypeStruct((2, 2, N, N), BF16),
            jax.ShapeDtypeStruct((2, 64, T), F32),
        ),
        in_specs=[anywhere, anywhere],
        out_specs=(anywhere,) * 8 + (vmem,) * 3,
        scratch_shapes=[
            pltpu.VMEM((2, 2, PACK, T), BF16),
            pltpu.VMEM((2, 4, 4, CHUNK, T), BF16),
            pltpu.VMEM((2, 4, 4, 2, 16, T), BF16),
            pltpu.VMEM((2, T, 2 * T), F32),
            pltpu.VMEM((2, N, N), F32),
            pltpu.VMEM((N, N), F32),
            pltpu.VMEM((2, N, N), BF16),
            dma((5,)), dma((2,)), dma((2, 3, 2)), dma((4, 3, 2)), dma((4, 2)), dma((4, PARTS, 2)), dma((3, PARTS, 2)),
        ],
        compiler_params=pltpu.CompilerParams(collective_id=0, has_side_effects=True, vmem_limit_bytes=40 << 20),
        cost_estimate=pl.CostEstimate(flops=4 * N**3, bytes_accessed=40 << 20, transcendentals=0),
    )(tiles, pack)


def place_of(q):
    return (q // 2) % COLS, (q // (2 * COLS)) * 2 + q % 2


def cols_kernel(src, at, p_ref, sinv_ref, out_ref):
    rows = jnp.concatenate([p_ref[0, 0, 0], p_ref[1, 0, 0]], axis=1)
    value = dot(sinv_ref[0, 0], rows, NT) + dot(sinv_ref[0, 1], rows, NT)
    high = value.astype(BF16)
    out_ref[0, 0] = high
    out_ref[0, 1] = (value - high.astype(F32)).astype(BF16)


def cols_factor(src, at, gathered, sinv):
    def p_map(l, j, src, at):
        parent = ((j // 2) * COLS + at[1]) * 2 + j % 2
        chip, slot = place_of(src[l * 64 + parent])
        return (0, chip, l, slot, 0)

    return pl.pallas_call(
        cols_kernel,
        name="cols_factor",
        out_shape=jax.ShapeDtypeStruct((2, 2, N, CHUNK), BF16),
        grid_spec=pltpu.PrefetchScalarGridSpec(
            num_scalar_prefetch=2,
            grid=(2, 4),
            in_specs=[
                pl.BlockSpec((2, 1, 1, T, T), p_map),
                pl.BlockSpec((1, 2, N, N), lambda l, j, src, at: (l, 0, 0, 0)),
            ],
            out_specs=pl.BlockSpec((1, 2, N, T), lambda l, j, src, at: (l, 0, 0, j)),
        ),
        cost_estimate=pl.CostEstimate(flops=8 * 4 * N * N * T, bytes_accessed=4 << 20, transcendentals=0),
    )(src, at, gathered, sinv)


def parent_kernel(src, at, *refs):
    data, (p_own, p_other, w_ref, reg_ref, out_ref, buf) = refs[:8], refs[8:]
    row, col, base, half = at[0], at[1], at[2], at[3]
    parent_row = 2 * (HALF * half + pl.program_id(0)) + row
    diagonal = lax.broadcasted_iota(jnp.int32, (T, T), 0) == lax.broadcasted_iota(jnp.int32, (T, T), 1)
    updates, from_rows = [], []
    for l in range(2):
        from_row = src[l * 64 + parent_row]
        from_rows.append(from_row)
        mine = from_row % 2 == row

        @pl.when(mine)
        def _():
            buf[l, :CHUNK] = data[4 * l][0].astype(F32)
            buf[l, CHUNK:] = data[4 * l + 1][0].astype(F32)

        @pl.when(jnp.logical_not(mine))
        def _():
            buf[l, :CHUNK] = data[4 * l + 2][0].astype(F32)
            buf[l, CHUNK:] = data[4 * l + 3][0].astype(F32)

        p_ref = (p_own, p_other)[l]
        rows = jnp.concatenate([p_ref[0, 0, 0], p_ref[1, 0, 0]], axis=1)
        updates.append(dot(rows, w_ref[l, 0], NN) + dot(rows, w_ref[l, 1], NN))
    for j in range(4):
        total = None
        for l in range(2):
            from_row = from_rows[l]
            from_col = src[l * 64 + ((j // 2) * COLS + col) * 2 + j % 2]
            chip, slot = place_of(from_col)
            span = pl.ds(jnp.where(chip == col, 0, CHUNK) + slot, T, stride=4)

            @pl.when(from_row == from_col)
            def _():
                buf[l, span, :] = buf[l, span, :] + jnp.where(diagonal, reg_ref[l, pl.ds(from_col, 1), :], 0.0)

            value = buf[l, span, :] - updates[l][:, j * T : (j + 1) * T]
            value = value.astype(BF16).astype(F32)
            value = jnp.where(jnp.logical_and(from_row > 0, from_col > 0), value, 0.0)
            total = value if total is None else total + value
        out_ref[0, pl.ds(j, T, stride=4), :] = total


def parent_out(src, at, data, gathered, weights, reg):
    def chunk_spec(l, partner, following):
        def index(i, src, at):
            q = src[l * 64 + 2 * (HALF * at[3] + i) + at[0]]
            wanted = (q % 2 == at[0]) != partner
            less = 0 if l == 0 and not partner and not following else at[2]
            return (jnp.where(wanted, jnp.maximum(q // 2 - less, 0), 0), 0, 0)

        return pl.BlockSpec((1, CHUNK, T), index)

    def p_spec(l):
        def index(i, src, at):
            chip, slot = place_of(src[l * 64 + 2 * (HALF * at[3] + i) + at[0]])
            return (0, chip, l, slot, 0)

        return pl.BlockSpec((2, 1, 1, T, T), index)

    return pl.pallas_call(
        parent_kernel,
        name="parent_out",
        out_shape=jax.ShapeDtypeStruct((HALF, CHUNK, T), F32),
        grid_spec=pltpu.PrefetchScalarGridSpec(
            num_scalar_prefetch=2,
            grid=(HALF,),
            in_specs=[chunk_spec(l, p, f) for l in range(2) for p in (False, True) for f in (False, True)]
            + [
                p_spec(0),
                p_spec(1),
                pl.BlockSpec((2, 2, N, CHUNK), lambda i, src, at: (0, 0, 0, 0)),
                pl.BlockSpec((2, 64, T), lambda i, src, at: (0, 0, 0)),
            ],
            out_specs=pl.BlockSpec((1, CHUNK, T), lambda i, src, at: (i, 0, 0)),
            scratch_shapes=[pltpu.VMEM((2, 2 * CHUNK, T), F32)],
        ),
        compiler_params=pltpu.CompilerParams(vmem_limit_bytes=32 << 20),
        cost_estimate=pl.CostEstimate(flops=2 * 2 * 4096 * N * CHUNK, bytes_accessed=14 << 20, transcendentals=0),
    )(src, at, *data, gathered, gathered, weights, reg)


def shards(front_tiles, regular, child_map):
    row, col = lax.axis_index("row"), lax.axis_index("col")
    half = lax.axis_index("leaf") % 2
    base = jnp.where(half == 0, 1, HALF)
    tiles = front_tiles.reshape(2 * COLS, CHUNK, T)

    columns = tiles[0].reshape(T, 4, T).transpose(1, 2, 0).reshape(CHUNK, T)
    gains = regular.reshape(2, T)
    high = lax.reduce_precision(gains, 8, 7)
    rest = gains - high
    middle = lax.reduce_precision(rest, 8, 7)
    pieces = jnp.concatenate([high, middle, rest - middle], axis=0).astype(BF16)
    parents = jnp.arange(64, dtype=jnp.int32)
    match = child_map.reshape(1, -1) == parents[:, None]
    source = jnp.sum(jnp.where(match, 2 + jnp.arange(62, dtype=jnp.int32)[None, :], 0), axis=1)
    source = jnp.pad(source, (0, T - 64)).astype(BF16)[None]
    pack = jnp.concatenate([columns, pieces, source, jnp.zeros((9, T), BF16)], axis=0)
    kn, oth, on, kx, knx, ox, onx, spread, panel, sinv, reg = exchange(tiles, pack)
    gathered = spread.reshape(2, COLS, 2, PACK, T)
    data = [tiles, kn, kx, knx, oth, on, ox, onx]
    src = gathered[0, 0, :, CHUNK + 6, :64].astype(jnp.int32).reshape(-1)
    at = jnp.stack([row, col, base, half]).astype(jnp.int32)

    weights = cols_factor(src, at, gathered, sinv)
    panel = panel.transpose(0, 1, 3, 2).reshape(1, 2, COLS, 1, T, 16)
    parent = parent_out(src, at, data, gathered, weights, reg)
    return panel, parent.reshape(1, 1, COLS, 1, T, 2, 1, 2, T)


def solution(mesh):
    return jax.shard_map(
        shards,
        mesh=mesh,
        in_specs=(
            P("leaf", None, None, "row", None, None, "col", None, None),
            P("leaf", None, "col", "row", None),
            P("leaf", None),
        ),
        out_specs=(
            P("leaf", None, None, "row", None, "col"),
            P("leaf", None, None, "row", None, None, "col", None, None),
        ),
        check_vma=False,
    )
```

time: 251 us -> 229 us (0.912)
  waiting for transfers between devices: 124 us -> 0 us
  Pallas kernels: 80.2 us -> 201 us
  starting transfers between devices: 14.7 us -> 0 us
  local copies, waits for them, and re-layouts: 8.4 us -> 22.9 us
  between operations: 14.2 us -> 0.73 us
  other arithmetic: 5.57 us -> 2.81 us
    pallas_call x2 -> x1, Pallas kernels: 54.6 us -> 177 us  [exchange(): pl.pallas_call(exchange_kernel, name='exchange', out_shape=(big,) * 7 + (...]
    ppermute x8 -> x0, waiting for transfers between devices: 92.4 us -> none  [the longest x6 47.3 us: swapped(): return lax.ppermute(value, axis, [(i, i ^ 1) for i in range(length)])]
    all_gather x1 -> x0, waiting for transfers between devices: 31.1 us -> none  [shards(): gathered = lax.all_gather(packs, ('row', 'col'), axis=0, tiled=False)]
    unnamed x14 -> x33, local copies, waits for them, and re-layouts: 3.46 us -> 21.1 us
    ppermute x8 -> x0, starting transfers between devices: 14.7 us -> none  [the longest x6 13.6 us: swapped(): return lax.ppermute(value, axis, [(i, i ^ 1) for i in range(length)])]
    dynamic_slice x1 -> x0, local copies, waits for them, and re-layouts: 2.57 us -> none  [shards(): send = lax.dynamic_slice_in_dim(tiles, HALF + 1 - base, HALF, 0)]
  transfers between devices with their start and end apart: 9 -> 0, of which waited for: 5 -> 0; matrix products, arithmetic and copies ran while one was open for 3% -> 0% of each run, Pallas kernels for 25% -> 0%
where the time goes in v2:
time: 229 us; the launch traced here: 227 us
  Pallas kernels  201 us (88%)
  local copies, waits for them, and re-layouts  22.9 us (10%)
  other arithmetic  2.81 us (1%)
    pallas_call x1, Pallas kernels, exchange(): pl.pallas_call(exchange_kernel, name='exchange', out_shape=(big,) * 7 + (...  177 us
    unnamed x33, local copies, waits for them, and re-layouts  21.1 us
    pallas_call x1, Pallas kernels, parent_out(): pl.pallas_call(parent_kernel, name='parent_out', out_shape=jax.ShapeDtype...  16.7 us
    pallas_call x1, Pallas kernels, cols_factor(): pl.pallas_call(cols_kernel, name='cols_factor', out_shape=jax.ShapeDtypeS...  7.01 us

profile of v2, /device:TPU:95, one launch (start us, length us, event | category | flops | bytes accessed | tf_op | source)
XLA Modules:
  0.0 227.1 jit_solution(6936683343578625668)
XLA Ops:
  0.6 0.7 pad_add_fusion.at
  1.3 0.8 select_reduce_fusion
  2.1 0.7 fusion
  2.8 0.9 slice.8
  3.7 0.1 copy.8
  3.8 0.2 concatenate.6.pack
  4.0 177.0 %exchange.1 = (bf16[16,512,128]{2,1,0:T(8,128)(2,1)S(1)}, bf16[16,512,128]{2,1,0:T(8,128)(2,1)S(1)}, bf16[16,512,128]{2,1,0:T(8,128)(2,1)S(1)}, bf16[16,512,128]...) custom-call(bf16[32,512,128]{2,1,0:T(8,128)(2,1)} %bitcast.23, ...), custom_call_target="tpu_custom_call" | custom-call | flops 67108864 | bytes 41943040 | tf_op jit(solution)/shard_map/exchange/pallas_call | solution.py:265
  181.0 0.0 copy-start.2
  181.0 1.3 copy-done.2
  182.3 0.0 copy-start.4
  182.3 1.3 copy-done.4
  183.6 0.0 copy-start.6
  183.6 1.3 copy-done.6
  184.9 0.0 copy-start.8
  184.9 1.3 copy-done.8
  186.3 0.0 copy-start.10
  186.3 1.3 copy-done.10
  187.6 0.0 copy-start.13
  187.6 0.8 copy-done.13
  188.4 0.7 fusion.1
  189.1 0.6 reshape.37.src
  189.7 0.0 copy-start.14
  189.7 0.0 copy-start.15
  189.7 7.0 %cols_factor.1.refs_10_ = bf16[2,2,256,512]{3,2,1,0:T(8,128)(2,1)} custom-call(s32[128]{0:T(128)} %reshape.37.src, s32[4]{0:T(128)} %pad_add_fusion.at, bf16[2,16,2,528,128]{4,3,2,1,0:T(8,128)(2,1)} %bitcast.27, bf16[2,2,256,256]{3,2,1,0:T(8,128)(2,1)} %copy-done.13), custom_call_target="tpu_custom_call" | custom-call | flops 268435456 | bytes 4194304 | tf_op jit(solution)/shard_map/cols_factor/pallas_call | solution.py:309
  196.7 0.0 copy-done.14
  196.7 0.0 copy-done.15
  196.7 0.0 copy-start
  196.8 2.2 copy-done
  198.9 0.0 copy-start.1
  198.9 1.2 copy-done.1
  200.2 0.0 copy-start.3
  200.2 1.6 copy-done.3
  201.7 0.0 copy-start.5
  201.8 1.6 copy-done.5
  203.3 0.0 copy-start.7
  203.3 1.6 copy-done.7
  204.9 0.0 copy-start.9
  204.9 1.6 copy-done.9
  206.5 0.0 copy-start.11
  206.5 1.6 copy-done.11
  208.1 0.0 copy-start.12
  208.1 1.6 copy-done.12
  209.7 16.7 %parent_out.1 = f32[16,512,128]{2,1,0:T(8,128)} custom-call(s32[128]{0:T(128)S(1)} %copy-done.15, s32[4]{0:T(128)S(1)} %copy-done.14, bf16[32,512,128]{2,1,0:T(8,128)(2,1)S(1)} %bitcast.24, bf16[16,512,128]{2,1,0:T(8,128)(2,1)S(1)} %get-tuple-element.15.refs_1_, bf16[16,512,128]{2,1,0:T(8,128)(2,1)S(1)} %copy-done.7, bf16[16,512,128]{2,1,0:T(8,128)(2,1)S(1)} %copy-done.9, ...), custom_call_target="tpu_custom_call" | custom-call | flops 2147483648 | bytes 14680064 | tf_op jit(solution)/shard_map/parent_out/pallas_call | solution.py:386
  226.4 0.7 copy.12
  (4 shorter events, 0.0 us)
Async XLA Ops:
  181.0 1.3 copy-start.2
  182.3 1.3 copy-start.4
  183.6 1.3 copy-start.6
  184.9 1.3 copy-start.8
  186.3 1.3 copy-start.10
  187.6 0.8 copy-start.13
  189.7 7.0 %copy-start.14 = (s32[4]{0:T(128)S(1)}, s32[4]{0:T(128)}, u32[]{:S(2)}) copy-start(s32[4]{0:T(128)} %pad_add_fusion.at) | copy-start | bytes 52
  189.7 7.0 %copy-start.15 = (s32[128]{0:T(128)S(1)}, s32[128]{0:T(128)}, u32[]{:S(2)}) copy-start(s32[128]{0:T(128)} %reshape.37.src) | copy-start | bytes 1540
  196.7 2.2 copy-start
  198.9 1.2 copy-start.1
  200.2 1.6 copy-start.3
  201.7 1.6 copy-start.5
  203.3 1.6 copy-start.7
  204.9 1.6 copy-start.9
  206.5 1.6 copy-start.11
  208.1 1.6 copy-start.12

commit v3 on v2

v3 whole, which is shorter than its diff:
```python
import jax
import jax.numpy as jnp
from jax import lax
from jax.experimental import pallas as pl
from jax.experimental.pallas import tpu as pltpu
from jax.sharding import PartitionSpec as P

T = 128
N = 256
COLS = 16
HALF = 16
CHUNK = 4 * T
BLOCK = 16
PACK = CHUNK + 16
HIGHEST = lax.Precision.HIGHEST
F32 = jnp.float32
BF16 = jnp.bfloat16


def dot(a, b, dims, precision=None):
    return lax.dot_general(a, b, (dims, ((), ())), precision=precision, preferred_element_type=F32)


NN = ((1,), (0,))
NT = ((1,), (1,))
TN = ((0,), (0,))


def unit_inverse(group, lane):
    a = {}
    for j in range(8):
        column = jnp.broadcast_to(group[:, lane + j : lane + j + 1], (8, T))
        for i in range(j, 8):
            a[i, j] = jnp.broadcast_to(column[i : i + 1, :], (8, T))
    low, inv = {}, {}
    for k in range(8):
        inv[k, k] = lax.rsqrt(a[k, k])
        for i in range(k + 1, 8):
            low[i, k] = a[i, k] * inv[k, k]
        for j in range(k + 1, 8):
            for i in range(j, 8):
                a[i, j] = a[i, j] - low[i, k] * low[j, k]
    for k in range(8):
        for i in range(k + 1, 8):
            total = low[i, k] * inv[k, k]
            for m in range(k + 1, i):
                total = total + low[i, m] * inv[m, k]
            inv[i, k] = -inv[i, i] * total
    return inv


def combined(weights, group):
    out = None
    for m in range(8):
        term = weights[m] * jnp.broadcast_to(group[m : m + 1, :], (8, T))
        out = term if out is None else out + term
    return out


def block_factor(rows, start):
    sub = lax.broadcasted_iota(jnp.int32, (8, T), 0)
    moved = pltpu.roll(rows[:, :T], lax.rem(T - start, T), axis=1)
    count = BLOCK // 8
    left = [moved[8 * g : 8 * g + 8] for g in range(count)]
    right = [rows[8 * g : 8 * g + 8, T:] for g in range(count)]
    for b in range(count):
        inv = unit_inverse(left[b], 8 * b)
        weights = []
        for m in range(8):
            weight = jnp.zeros((8, T), F32)
            for k in range(m, 8):
                weight = jnp.where(sub == k, inv[k, m], weight)
            weights.append(weight)
        left_next, right_next = combined(weights, left[b]), combined(weights, right[b])
        for g in range(b + 1, count):
            columns = [jnp.broadcast_to(left[g][:, 8 * b + k : 8 * b + k + 1], (8, T)) for k in range(8)]
            lows = []
            for m in range(8):
                low = columns[0] * inv[m, 0]
                for k in range(1, m + 1):
                    low = low + columns[k] * inv[m, k]
                lows.append(low)
            left[g] = left[g] - combined(lows, left_next)
            right[g] = right[g] - combined(lows, right_next)
        left[b], right[b] = left_next, right_next
    upper = pltpu.roll(jnp.concatenate(left, axis=0), start, axis=1)
    lane = lax.broadcasted_iota(jnp.int32, (BLOCK, T), 1)
    upper = jnp.where(lane >= start + lax.broadcasted_iota(jnp.int32, (BLOCK, T), 0), upper, 0.0)
    later = jnp.where(lane >= start + BLOCK, upper, 0.0)
    return jnp.concatenate([upper, jnp.concatenate(right, axis=0)], axis=1), later


def split(value):
    high = value.astype(BF16)
    return high, (value - high.astype(F32)).astype(BF16)


def eliminate(work, hooks):
    def body(b, carry):
        start = pl.multiple_of(b * BLOCK, BLOCK)
        done = [block_factor(work[l, pl.ds(start, BLOCK), :], start) for l in range(2)]
        for l in range(2):
            rows, later = done[l]
            high, low = split(rows)
            later_high, later_low = split(later)
            left = jnp.concatenate([later_high, later_high, later_low], axis=0)
            right = jnp.concatenate([high, low, high], axis=0)
            work[l] = work[l] - dot(left, right, TN)
            work[l, pl.ds(start, BLOCK), :] = rows
        return carry

    count, steps = len(hooks), T // BLOCK
    for n, hook in enumerate(hooks):
        lax.fori_loop(n * steps // count, (n + 1) * steps // count, body, 0)
        hook()


def factor(top, work, full, upper, linv, sinv, hooks):
    eye = lax.broadcasted_iota(jnp.int32, (T, T), 0) == lax.broadcasted_iota(jnp.int32, (T, T), 1)
    one = jnp.where(eye, 1.0, 0.0).astype(F32)

    def block(q, s, l):
        value = top[s, l, q * T : (q + 1) * T, :].astype(F32)
        if q == s:
            parts = top[s, l, N : N + 16, :].astype(F32)
            gain = (parts[0:1] + parts[2:3]) + parts[4:5]
            value = value + jnp.where(eye, gain, 0.0)
        return value

    for l in range(2):
        work[l, :, :T] = block(0, 0, l)
        work[l, :, T:] = one
    eliminate(work, hooks[0])
    for l in range(2):
        inverse = work[l, :, T:]
        across = dot(inverse, block(0, 1, l), NN, HIGHEST)
        if l == 0:
            upper[:, :T] = jnp.concatenate([work[l, :, :T], jnp.zeros((T, T), F32)], axis=0)
            upper[:T, T:] = across
        full[l, :T, :T] = inverse
        full[l, :T, T:] = jnp.zeros((T, T), F32)
        full[l, T:, :T] = dot(across, inverse, TN, HIGHEST)
        work[l, :, :T] = block(1, 1, l) - dot(across, across, TN, HIGHEST)
        work[l, :, T:] = one
    eliminate(work, hooks[1])
    for l in range(2):
        inverse = work[l, :, T:]
        if l == 0:
            upper[T:, T:] = work[l, :, :T]
        full[l, T:, :T] = -dot(inverse, full[l, T:, :T], NN, HIGHEST)
        full[l, T:, T:] = inverse
        whole = full[l]
        sinv[l, 0], sinv[l, 1] = split(dot(whole, whole, TN, HIGHEST))
    linv[0], linv[1] = split(full[0])


PARTS = 4
FORWARDED = 1
ROWS = HALF // PARTS
MESH = pl.DeviceIdType.MESH


def exchange_kernel(
    tiles, regular, cmap, kn, oth, on, kx, knx, ox, onx, spread, panel, weights, reg,
    pack, raw, wide, top, own, cand, gains, work, full, upper, linv, sinv,
    local_sem, z_sem, lane_sem, lane_core_sem, ring_sem, core_sem, bulk_sem, pass_sem,
):
    leaf, row, col = lax.axis_index("leaf"), lax.axis_index("row"), lax.axis_index("col")
    y, x = col // 4, col % 4
    sibling = leaf + 1 - 2 * (leaf % 2)
    before, after = lax.rem(col + COLS - 1, COLS), lax.rem(col + 1, COLS)
    half = leaf % 2
    keep = 1 + half * (HALF - 1)
    send = HALF - half * (HALF - 1)
    across = (leaf, 1 - row, col)
    x_next = (leaf, row, y * 4 + lax.rem(x + 1, 4))
    y_next = (leaf, row, lax.rem(y + 1, 4) * 4 + x)

    peers = [(sibling, row, col), (sibling, row, before), (sibling, row, after)]
    peers += [(leaf, row, before), (leaf, row, after), across]
    peers += [(leaf, row, y * 4 + lax.rem(x + d, 4)) for d in (1, 3)]
    peers += [(leaf, row, lax.rem(y + d, 4) * 4 + x) for d in (1, 3)]
    first_rows = pltpu.make_async_copy(tiles.at[0], raw, local_sem.at[0])
    first_rows.start()
    barrier = pltpu.get_barrier_semaphore()
    for peer in peers:
        pl.semaphore_signal(barrier, inc=1, device_id=peer, device_id_type=MESH)
    pl.semaphore_wait(barrier, len(peers))

    def remote(source, target, sems, peer):
        return pltpu.make_async_remote_copy(
            src_ref=source, dst_ref=target, send_sem=sems.at[0], recv_sem=sems.at[1],
            device_id=peer, device_id_type=MESH,
        )

    sent = []

    def start(copy):
        copy.start()
        sent.append(copy)
        return copy

    def hop(stage, step):
        l = stage % 2
        along_x = (stage // 2) == l
        origin = lax.rem((x if along_x else y) + 4 - step, 4)
        if stage < 2:
            place = spread.at[row, y, origin, l] if along_x else spread.at[row, origin, x, l]
        else:
            place = spread.at[row, :, origin, l] if along_x else spread.at[row, origin, :, l]
        source = pack if stage == 0 and step == 0 else place
        return start(remote(source, place, ring_sem.at[stage, step], x_next if along_x else y_next))

    bulk = []
    for k in range(PARTS):
        kept, part = tiles.at[pl.ds(keep + k * ROWS, ROWS)], pl.ds(k * ROWS, ROWS)
        bulk.append([
            start(remote(kept, kn.at[part], bulk_sem.at[0, k], (leaf, row, before))),
            start(remote(kept, kx.at[part], bulk_sem.at[3, k], across)),
        ])

    first_rows.wait()
    wide[...] = raw[...].astype(F32)
    for j in range(4):
        pack[j * T : (j + 1) * T, :] = wide[pl.ds(j, T, stride=4), :].T.astype(BF16)
    value = regular[...]
    high = value.astype(BF16).astype(F32)
    rest = value - high
    middle = rest.astype(BF16).astype(F32)
    lane = lax.broadcasted_iota(jnp.int32, (T, T), 1)
    match = cmap[...] == lax.broadcasted_iota(jnp.int32, (T, T), 0)
    source = jnp.where(match, lane + 2, 0).astype(F32).T
    source = jnp.sum(source, axis=0, keepdims=True)
    pack[CHUNK:, :] = jnp.concatenate([high, middle, rest - middle, source, jnp.zeros((9, T), F32)], axis=0).astype(BF16)

    to_sibling = start(remote(pack, spread.at[row, y, x, 1], z_sem, (sibling, row, col)))
    last = [hop(0, 0), None]
    place = pltpu.make_async_copy(pack, spread.at[row, y, x, 0], local_sem.at[0])
    place.start()
    for k in range(PARTS):
        gone, part = tiles.at[pl.ds(send + k * ROWS, ROWS)], pl.ds(k * ROWS, ROWS)
        bulk[k].insert(1, start(remote(gone, oth.at[part], bulk_sem.at[1, k], (sibling, row, col))))
        if k >= FORWARDED:
            bulk[k].insert(2, start(remote(gone, on.at[part], bulk_sem.at[2, k], (sibling, row, before))))

    def forward():
        for k in range(FORWARDED):
            part = pl.ds(k * ROWS, ROWS)
            bulk[k][1].wait_recv()
            bulk[k].insert(2, start(remote(oth.at[part], on.at[part], bulk_sem.at[2, k], (leaf, row, before))))

    to_sibling.wait_recv()
    last[1] = hop(1, 0)

    core_copies = []

    def over_core(l, step):
        origin = lax.rem((x if l else y) + 4 - step, 4)
        group = spread.at[row, :, origin, l] if l else spread.at[row, origin, :, l]
        core_copies.append(start(remote(group, group, core_sem.at[l, step], across)))

    def relay(stage, step):
        l = stage % 2
        last[l].wait_recv()
        last[l] = hop(stage, step)
        if stage >= 2:
            over_core(l, step)

    @pl.when(col == 0)
    def _():
        loads = []
        for l in range(2):
            origin = pack if l == 0 else spread.at[row, y, x, 1]
            loads.append(pltpu.make_async_copy(
                origin.at[pl.ds(0, N)], top.at[row, l, pl.ds(0, N)], local_sem.at[1 + l]))
            loads.append(pltpu.make_async_copy(
                origin.at[pl.ds(CHUNK, 16)], top.at[row, l, pl.ds(N, 16)], local_sem.at[3 + l]))
        for load in loads:
            load.start()
        for load in loads:
            load.wait()

    def lane(n, peer):
        return pltpu.make_async_remote_copy(
            src_ref=top.at[row], dst_ref=top.at[row], send_sem=lane_sem.at[n], recv_sem=lane_sem.at[2],
            device_id=peer, device_id_type=MESH)

    lane_x, lane_y = lane(0, x_next), lane(1, y_next)

    @pl.when(jnp.logical_and(y == 0, x > 0))
    def _():
        lane_x.wait_recv()

    @pl.when(jnp.logical_and(y == 0, x < 3))
    def _():
        lane_x.start()

    @pl.when(y == 0)
    def _():
        lane_y.start()

    for step in (1, 2):
        relay(0, step)
        relay(1, step)

        @pl.when(y == step)
        def _():
            lane_y.wait_recv()
            lane_y.start()

    place.wait()
    relay(2, 0)
    relay(3, 0)

    @pl.when(y == 3)
    def _():
        lane_y.wait_recv()

    lane_core = start(remote(top.at[row], top.at[row], lane_core_sem, across))
    lane_core.wait_recv()

    def nothing():
        pass

    def both(step):
        relay(2, step)
        relay(3, step)

    hooks = ([forward, nothing, nothing, nothing], [nothing, lambda: both(1), nothing, nothing])
    factor(top, work, full, upper, linv, sinv, hooks)
    both(2)
    for l in range(2):
        last[l].wait_recv()
        over_core(l, 3)
    for copy in core_copies:
        copy.wait_recv()
    ay, ax = after // 4, lax.rem(after, 4)
    loads = [
        pltpu.make_async_copy(spread.at[:, :, :, 0, pl.ds(0, CHUNK)], own, local_sem.at[0]),
        pltpu.make_async_copy(spread.at[:, :, :, :, pl.ds(CHUNK, 16)], gains, local_sem.at[1]),
        pltpu.make_async_copy(spread.at[:, y, x, :, pl.ds(0, CHUNK)], cand.at[0], local_sem.at[2]),
        pltpu.make_async_copy(spread.at[:, ay, ax, :, pl.ds(0, CHUNK)], cand.at[1], local_sem.at[3]),
    ]
    for load in loads:
        load.start()
    for load in loads:
        load.wait()

    def candidate(n, carry):
        which, slot = n // 4, n % 4
        span = pl.ds(pl.multiple_of(slot * T, T), T)
        for l in range(2):
            rows = jnp.concatenate([cand[which, 0, l, span, :], cand[which, 1, l, span, :]], axis=1)
            value = dot(sinv[l, 0], rows, NT) + dot(sinv[l, 1], rows, NT)
            weights[n, l, 0], weights[n, l, 1] = split(value)
        return carry

    lax.fori_loop(0, 8, candidate, 0)

    first = pl.multiple_of(col * 16, 16)
    slices = jnp.concatenate([linv[0, pl.ds(first, 16), :], linv[1, pl.ds(first, 16), :]], axis=0)

    def chip(at, carry):
        cy, cx = at // 4, at % 4
        for o in range(2):
            span = pl.ds(pl.multiple_of((o * 2 + row) * T, T), T)
            rows = jnp.concatenate([own[0, cy, cx, span, :], own[1, cy, cx, span, :]], axis=1)
            pair = dot(slices, rows, NT)
            panel[o, at] = pair[:16] + pair[16:]
        for s in range(2):
            for l in range(2):
                parts = gains[s, cy, cx, l].astype(F32)
                for o in range(2):
                    gain = (parts[o : o + 1] + parts[2 + o : 3 + o]) + parts[4 + o : 5 + o]
                    reg[l, pl.ds((o * COLS + at) * 2 + s, 1), :] = gain
        return carry

    lax.fori_loop(0, COLS, chip, 0)
    panel[0, 0] = upper[pl.ds(first, 16), pl.ds(pl.multiple_of(row * T, T), T)]

    passed = []
    for k in range(PARTS):
        part = pl.ds(k * ROWS, ROWS)
        for n, (source, target) in enumerate(((kn, knx), (oth, ox), (on, onx))):
            if n != 1 or k >= FORWARDED:
                bulk[k][n].wait_recv()
            passed.append(start(remote(source.at[part], target.at[part], pass_sem.at[n, k], across)))
    for k in range(PARTS):
        bulk[k][3].wait_recv()
    for copy in passed:
        copy.wait_recv()
    for copy in sent:
        copy.wait_send()

    @pl.when(jnp.logical_and(y == 0, x < 3))
    def _():
        lane_x.wait_send()

    @pl.when(y < 3)
    def _():
        lane_y.wait_send()


def exchange(tiles, regular, cmap):
    big = jax.ShapeDtypeStruct((HALF, CHUNK, T), BF16)
    spread = jax.ShapeDtypeStruct((2, 4, 4, 2, PACK, T), BF16)
    dma = pltpu.SemaphoreType.DMA
    anywhere, vmem = pl.BlockSpec(memory_space=pltpu.HBM), pl.BlockSpec(memory_space=pltpu.VMEM)
    return pl.pallas_call(
        exchange_kernel,
        name="exchange",
        out_shape=(big,) * 7 + (
            spread,
            jax.ShapeDtypeStruct((2, COLS, 16, T), F32),
            jax.ShapeDtypeStruct((8, 2, 2, N, T), BF16),
            jax.ShapeDtypeStruct((2, 64, T), F32),
        ),
        in_specs=[anywhere, vmem, vmem],
        out_specs=(anywhere,) * 8 + (vmem,) * 3,
        scratch_shapes=[
            pltpu.VMEM((PACK, T), BF16),
            pltpu.VMEM((CHUNK, T), BF16),
            pltpu.VMEM((CHUNK, T), F32),
            pltpu.VMEM((2, 2, N + 16, T), BF16),
            pltpu.VMEM((2, 4, 4, CHUNK, T), BF16),
            pltpu.VMEM((2, 2, 2, CHUNK, T), BF16),
            pltpu.VMEM((2, 4, 4, 2, 16, T), BF16),
            pltpu.VMEM((2, T, 2 * T), F32),
            pltpu.VMEM((2, N, N), F32),
            pltpu.VMEM((N, N), F32),
            pltpu.VMEM((2, N, N), BF16),
            pltpu.VMEM((2, 2, N, N), BF16),
            dma((5,)), dma((2,)), dma((3,)), dma((2,)), dma((4, 3, 2)), dma((2, 4, 2)), dma((4, PARTS, 2)), dma((3, PARTS, 2)),
        ],
        compiler_params=pltpu.CompilerParams(collective_id=0, has_side_effects=True, vmem_limit_bytes=56 << 20),
        cost_estimate=pl.CostEstimate(flops=4 * N**3, bytes_accessed=40 << 20, transcendentals=0),
    )(tiles, regular, cmap)


def place_of(q):
    return (q // 2) % COLS, (q // (2 * COLS)) * 2 + q % 2


PAIR = 2


def parent_kernel(src, at, *refs):
    data, p_refs = refs[: 8 * PAIR], refs[8 * PAIR : 10 * PAIR]
    w_ref, reg_ref, out_ref, buf = refs[10 * PAIR :]
    row, col, half = at[0], at[1], at[3]
    diagonal = lax.broadcasted_iota(jnp.int32, (T, T), 0) == lax.broadcasted_iota(jnp.int32, (T, T), 1)
    from_rows, from_cols, spans, updates = {}, {}, {}, []
    for l in range(2):
        picks = []
        for j in range(4):
            from_col = src[l * 64 + ((j // 2) * COLS + col) * 2 + j % 2]
            chip, slot = place_of(from_col)
            far = jnp.where(chip == col, 0, 1)
            from_cols[l, j] = from_col
            spans[l, j] = pl.ds(far * CHUNK + slot, T, stride=4)
            picks.append(far * 4 + slot)
        rows = []
        for r in range(PAIR):
            from_row = src[l * 64 + 2 * (HALF * half + PAIR * pl.program_id(0) + r) + row]
            from_rows[l, r] = from_row
            mine = from_row % 2 == row
            part = data[8 * r + 4 * l : 8 * r + 4 * l + 4]

            @pl.when(mine)
            def _():
                buf[l, r, :CHUNK] = part[0][0].astype(F32)
                buf[l, r, CHUNK:] = part[1][0].astype(F32)

            @pl.when(jnp.logical_not(mine))
            def _():
                buf[l, r, :CHUNK] = part[2][0].astype(F32)
                buf[l, r, CHUNK:] = part[3][0].astype(F32)

            p_ref = p_refs[2 * r + l]
            rows.append(jnp.concatenate([p_ref[0, 0, 0], p_ref[1, 0, 0]], axis=1))
            for j in range(4):

                @pl.when(from_row == from_cols[l, j])
                def _():
                    gain = reg_ref[l, pl.ds(from_row, 1), :]
                    buf[l, r, spans[l, j], :] = buf[l, r, spans[l, j], :] + jnp.where(diagonal, gain, 0.0)

        rows = jnp.concatenate(rows, axis=0)
        high = jnp.concatenate([w_ref[pick, l, 0] for pick in picks], axis=1)
        low = jnp.concatenate([w_ref[pick, l, 1] for pick in picks], axis=1)
        updates.append(dot(rows, high, NN) + dot(rows, low, NN))
    for r in range(PAIR):
        for j in range(4):
            total = None
            for l in range(2):
                value = buf[l, r, spans[l, j], :] - updates[l][r * T : (r + 1) * T, j * T : (j + 1) * T]
                value = value.astype(BF16).astype(F32)
                value = jnp.where(jnp.logical_and(from_rows[l, r] > 0, from_cols[l, j] > 0), value, 0.0)
                total = value if total is None else total + value
            out_ref[r, pl.ds(j, T, stride=4), :] = total


def parent_out(src, at, data, gathered, weights, reg):
    def source(i, r, l, src, at):
        return src[l * 64 + 2 * (HALF * at[3] + PAIR * i + r) + at[0]]

    def chunk_spec(r, l, partner, following):
        def index(i, src, at):
            q = source(i, r, l, src, at)
            wanted = (q % 2 == at[0]) != partner
            less = 0 if l == 0 and not partner and not following else at[2]
            return (jnp.where(wanted, jnp.maximum(q // 2 - less, 0), 0), 0, 0)

        return pl.BlockSpec((1, CHUNK, T), index)

    def p_spec(r, l):
        def index(i, src, at):
            chip, slot = place_of(source(i, r, l, src, at))
            return (0, chip, l, slot, 0)

        return pl.BlockSpec((2, 1, 1, T, T), index)

    pairs = [(r, l) for r in range(PAIR) for l in range(2)]
    return pl.pallas_call(
        parent_kernel,
        name="parent_out",
        out_shape=jax.ShapeDtypeStruct((HALF, CHUNK, T), F32),
        grid_spec=pltpu.PrefetchScalarGridSpec(
            num_scalar_prefetch=2,
            grid=(HALF // PAIR,),
            in_specs=[chunk_spec(r, l, p, f) for r, l in pairs for p in (False, True) for f in (False, True)]
            + [p_spec(r, l) for r, l in pairs]
            + [
                pl.BlockSpec((8, 2, 2, N, T), lambda i, src, at: (0, 0, 0, 0, 0)),
                pl.BlockSpec((2, 64, T), lambda i, src, at: (0, 0, 0)),
            ],
            out_specs=pl.BlockSpec((PAIR, CHUNK, T), lambda i, src, at: (i, 0, 0)),
            scratch_shapes=[pltpu.VMEM((2, PAIR, 2 * CHUNK, T), F32)],
        ),
        compiler_params=pltpu.CompilerParams(vmem_limit_bytes=56 << 20),
        cost_estimate=pl.CostEstimate(flops=2 * 2 * 4096 * N * CHUNK, bytes_accessed=14 << 20, transcendentals=0),
    )(src, at, *(data * PAIR), *([gathered] * (2 * PAIR)), weights, reg)


def shards(front_tiles, regular, child_map):
    row, col = lax.axis_index("row"), lax.axis_index("col")
    half = lax.axis_index("leaf") % 2
    base = jnp.where(half == 0, 1, HALF)
    tiles = front_tiles.reshape(2 * COLS, CHUNK, T)

    cmap = jnp.pad(child_map, ((0, 0), (0, T - child_map.shape[1])), constant_values=-1)
    kn, oth, on, kx, knx, ox, onx, spread, panel, weights, reg = exchange(tiles, regular.reshape(2, T), cmap)
    gathered = spread.reshape(2, COLS, 2, PACK, T)
    data = [tiles, kn, kx, knx, oth, on, ox, onx]
    src = gathered[0, 0, :, CHUNK + 6, :64].astype(jnp.int32).reshape(-1)
    at = jnp.stack([row, col, base, half]).astype(jnp.int32)

    panel = panel.transpose(0, 1, 3, 2).reshape(1, 2, COLS, 1, T, 16)
    parent = parent_out(src, at, data, gathered, weights, reg)
    return panel, parent.reshape(1, 1, COLS, 1, T, 2, 1, 2, T)


def solution(mesh):
    return jax.shard_map(
        shards,
        mesh=mesh,
        in_specs=(
            P("leaf", None, None, "row", None, None, "col", None, None),
            P("leaf", None, "col", "row", None),
            P("leaf", None),
        ),
        out_specs=(
            P("leaf", None, None, "row", None, "col"),
            P("leaf", None, None, "row", None, None, "col", None, None),
        ),
        check_vma=False,
    )
```

time: 229 us -> 134 us (0.59)
  Pallas kernels: 201 us -> 129 us
  local copies, waits for them, and re-layouts: 22.9 us -> 2.47 us
    pallas_call x1, Pallas kernels: 177 us -> 110 us  [exchange(): pl.pallas_call(exchange_kernel, name='exchange', out_shape=(big,) * 7 + (...]
    unnamed x33 -> x3, local copies, waits for them, and re-layouts: 21.1 us -> 0.71 us
    pallas_call x1 -> x0, Pallas kernels: 7.01 us -> none  [cols_factor(): pl.pallas_call(cols_kernel, name='cols_factor', out_shape=jax.ShapeDtypeS...]
    pallas_call x1, Pallas kernels: 16.7 us -> 19.4 us  [parent_out(): pl.pallas_call(parent_kernel, name='parent_out', out_shape=jax.ShapeDtype...]
where the time goes in v3:
time: 134 us
  Pallas kernels  129 us (96%)
  local copies, waits for them, and re-layouts  2.47 us (2%)
    pallas_call x1, Pallas kernels, exchange(): pl.pallas_call(exchange_kernel, name='exchange', out_shape=(big,) * 7 + (...  110 us
    pallas_call x1, Pallas kernels, parent_out(): pl.pallas_call(parent_kernel, name='parent_out', out_shape=jax.ShapeDtype...  19.4 us

profile of v3, /device:TPU:95, one launch (start us, length us, event | category | flops | bytes accessed | tf_op | source)
XLA Modules:
  0.0 133.5 jit_solution(10920605261261598709)
XLA Ops:
  0.6 0.6 pad_add_fusion.at
  1.2 1.2 pad.4.cmap
  2.4 109.7 %exchange.1 = (bf16[16,512,128]{2,1,0:T(8,128)(2,1)}, bf16[16,512,128]{2,1,0:T(8,128)(2,1)}, bf16[16,512,128]{2,1,0:T(8,128)(2,1)}, bf16[16,512,128]{2,1,0:T(8,1...) custom-call(bf16[32,512,128]{2,1,0:T(8,128)(2,1)} %bitcast.20, ...), custom_call_target="tpu_custom_call" | custom-call | flops 67108864 | bytes 41943040 | tf_op jit(solution)/shard_map/exchange/pallas_call | solution.py:409
  112.1 0.7 fusion
  112.8 0.6 reshape.28.src
  113.3 0.0 copy-start
  113.4 19.4 %parent_out.1 = f32[16,512,128]{2,1,0:T(8,128)} custom-call(s32[128]{0:T(128)} %reshape.28.src, s32[4]{0:T(128)} %pad_add_fusion.at, bf16[32,512,128]{2,1,0:T(8,128)(2,1)} %bitcast.21, bf16[16,512,128]{2,1,0:T(8,128)(2,1)} %get-tuple-element.15.refs_1_.refs_9_, bf16[16,512,128]{2,1,0:T(8,128)(2,1)} %get-tuple-element.16.refs_2_.refs_10_, ...), custom_call_target="tpu_custom_call" | custom-call | flops 2147483648 | bytes 14680064 | tf_op jit(solution)/shard_map/parent_out/pallas_call | solution.py:524
  132.8 0.0 copy-done
  132.8 0.7 copy.8
Async XLA Ops:
  113.3 19.4 %copy-start = (f32[2,16,16,128]{3,2,1,0:T(8,128)S(1)}, f32[2,16,16,128]{3,2,1,0:T(8,128)}, u32[]{:S(2)}) copy-start(f32[2,16,16,128]{3,2,1,0:T(8,128)} %get-tuple-element.13) | copy-start | bytes 786436

commit v4 on v3

--- a/solution.py
+++ b/solution.py
@@ -329,14 +329,41 @@
     hooks = ([forward, nothing, nothing, nothing], [nothing, lambda: both(1), nothing, nothing])
     factor(top, work, full, upper, linv, sinv, hooks)
     both(2)
+    first = pl.multiple_of(col * 16, 16)
+    slices = jnp.concatenate([linv[0, pl.ds(first, 16), :], linv[1, pl.ds(first, 16), :]], axis=0)
+
+    def panel_groups(steps):
+        loads = []
+        for n, step in enumerate(steps):
+            cy = lax.rem(y + 4 - step, 4)
+            load = pltpu.make_async_copy(spread.at[:, cy, :, 0, pl.ds(0, CHUNK)], own.at[:, cy], local_sem.at[n])
+            load.start()
+            loads.append(load)
+        for load in loads:
+            load.wait()
+
+        def chip(n, carry):
+            cy, cx = lax.rem(y + 4 - (steps[0] + n // 4), 4), n % 4
+            for o in range(2):
+                span = pl.ds(pl.multiple_of((o * 2 + row) * T, T), T)
+                rows = jnp.concatenate([own[0, cy, cx, span, :], own[1, cy, cx, span, :]], axis=1)
+                pair = dot(slices, rows, NT)
+                panel[o, cy * 4 + cx] = pair[:16] + pair[16:]
+            return carry
+
+        lax.fori_loop(0, 4 * len(steps), chip, 0)
+
+    for copy in core_copies:
+        copy.wait_recv()
+    panel_groups((0, 1, 2))
     for l in range(2):
         last[l].wait_recv()
         over_core(l, 3)
-    for copy in core_copies:
+    for copy in core_copies[6:]:
         copy.wait_recv()
+    panel_groups((3,))
     ay, ax = after // 4, lax.rem(after, 4)
     loads = [
-        pltpu.make_async_copy(spread.at[:, :, :, 0, pl.ds(0, CHUNK)], own, local_sem.at[0]),
         pltpu.make_async_copy(spread.at[:, :, :, :, pl.ds(CHUNK, 16)], gains, local_sem.at[1]),
         pltpu.make_async_copy(spread.at[:, y, x, :, pl.ds(0, CHUNK)], cand.at[0], local_sem.at[2]),
         pltpu.make_async_copy(spread.at[:, ay, ax, :, pl.ds(0, CHUNK)], cand.at[1], local_sem.at[3]),
@@ -357,16 +384,8 @@
 
     lax.fori_loop(0, 8, candidate, 0)
 
-    first = pl.multiple_of(col * 16, 16)
-    slices = jnp.concatenate([linv[0, pl.ds(first, 16), :], linv[1, pl.ds(first, 16), :]], axis=0)
-
-    def chip(at, carry):
+    def chip_gains(at, carry):
         cy, cx = at // 4, at % 4
-        for o in range(2):
-            span = pl.ds(pl.multiple_of((o * 2 + row) * T, T), T)
-            rows = jnp.concatenate([own[0, cy, cx, span, :], own[1, cy, cx, span, :]], axis=1)
-            pair = dot(slices, rows, NT)
-            panel[o, at] = pair[:16] + pair[16:]
         for s in range(2):
             for l in range(2):
                 parts = gains[s, cy, cx, l].astype(F32)
@@ -375,7 +394,7 @@
                     reg[l, pl.ds((o * COLS + at) * 2 + s, 1), :] = gain
         return carry
 
-    lax.fori_loop(0, COLS, chip, 0)
+    lax.fori_loop(0, COLS, chip_gains, 0)
     panel[0, 0] = upper[pl.ds(first, 16), pl.ds(pl.multiple_of(row * T, T), T)]
 
     passed = []
@@ -438,10 +457,10 @@
 
 
 def place_of(q):
-    return (q // 2) % COLS, (q // (2 * COLS)) * 2 + q % 2
-
-
-PAIR = 2
+    return (q >> 1) & (COLS - 1), ((q >> 5) << 1) + (q & 1)
+
+
+PAIR = 4
 
 
 def parent_kernel(src, at, *refs):
@@ -463,7 +482,7 @@
         for r in range(PAIR):
             from_row = src[l * 64 + 2 * (HALF * half + PAIR * pl.program_id(0) + r) + row]
             from_rows[l, r] = from_row
-            mine = from_row % 2 == row
+            mine = (from_row & 1) == row
             part = data[8 * r + 4 * l : 8 * r + 4 * l + 4]
 
             @pl.when(mine)
@@ -507,9 +526,9 @@
     def chunk_spec(r, l, partner, following):
         def index(i, src, at):
             q = source(i, r, l, src, at)
-            wanted = (q % 2 == at[0]) != partner
+            wanted = (q & 1) == (at[0] ^ int(partner))
             less = 0 if l == 0 and not partner and not following else at[2]
-            return (jnp.where(wanted, jnp.maximum(q // 2 - less, 0), 0), 0, 0)
+            return (jnp.where(wanted, jnp.maximum((q >> 1) - less, 0), 0), 0, 0)
 
         return pl.BlockSpec((1, CHUNK, T), index)
 

time: 134 us -> 130 us (0.970)
  Pallas kernels: 129 us -> 126 us
    pallas_call x1, Pallas kernels: 19.4 us -> 16 us  [parent_out(): pl.pallas_call(parent_kernel, name='parent_out', out_shape=jax.ShapeDtype...]
where the time goes in v4:
time: 130 us
  Pallas kernels  126 us (97%)
  local copies, waits for them, and re-layouts  2.47 us (2%)
    pallas_call x1, Pallas kernels, exchange(): pl.pallas_call(exchange_kernel, name='exchange', out_shape=(big,) * 7 + (...  110 us
    pallas_call x1, Pallas kernels, parent_out(): pl.pallas_call(parent_kernel, name='parent_out', out_shape=jax.ShapeDtype...  16 us

profile of v4, /device:TPU:95, one launch (start us, length us, event | category | flops | bytes accessed | tf_op | source)
XLA Modules:
  0.0 130.0 jit_solution(7091720280759701181)
XLA Ops:
  0.6 0.6 pad_add_fusion.at
  1.2 1.2 pad.4.cmap
  2.4 109.7 %exchange.1 = (bf16[16,512,128]{2,1,0:T(8,128)(2,1)}, bf16[16,512,128]{2,1,0:T(8,128)(2,1)}, bf16[16,512,128]{2,1,0:T(8,128)(2,1)}, bf16[16,512,128]{2,1,0:T(8,1...) custom-call(bf16[32,512,128]{2,1,0:T(8,128)(2,1)} %bitcast.24, ...), custom_call_target="tpu_custom_call" | custom-call | flops 67108864 | bytes 41943040 | tf_op jit(solution)/shard_map/exchange/pallas_call | solution.py:428
  112.1 0.7 fusion
  112.8 0.6 reshape.28.src
  113.3 0.0 copy-start
  113.4 16.0 %parent_out.1 = f32[16,512,128]{2,1,0:T(8,128)} custom-call(s32[128]{0:T(128)} %reshape.28.src, s32[4]{0:T(128)} %pad_add_fusion.at, bf16[32,512,128]{2,1,0:T(8,128)(2,1)} %bitcast.25, bf16[16,512,128]{2,1,0:T(8,128)(2,1)} %get-tuple-element.15.refs_1_.refs_9_.refs_17_.refs_25_, bf16[16,512,128]{2,1,0:T(8,128)(2,1)} %get-tuple-element.16.refs_2_.refs_10_.refs_18_.refs_26_, ...), custom_call_target="tpu_custom_call" | custom-call | flops 2147483648 | bytes 14680064 | tf_op jit(solution)/shard_map/parent_out/pallas_call | solution.py:543
  129.3 0.0 copy-done
  129.3 0.7 copy.8
Async XLA Ops:
  113.3 16.0 %copy-start = (f32[2,16,16,128]{3,2,1,0:T(8,128)S(1)}, f32[2,16,16,128]{3,2,1,0:T(8,128)}, u32[]{:S(2)}) copy-start(f32[2,16,16,128]{3,2,1,0:T(8,128)} %get-tuple-element.13) | copy-start | bytes 786436

commit v5 on v4

--- a/solution.py
+++ b/solution.py
@@ -155,7 +155,7 @@
 
 
 PARTS = 4
-FORWARDED = 1
+FORWARDED = 3
 ROWS = HALF // PARTS
 MESH = pl.DeviceIdType.MESH
 

time: 130 us -> 127 us (0.977); the launches traced: 130 us -> 126 us
  Pallas kernels: 126 us -> 121 us
    pallas_call x1, Pallas kernels: 110 us -> 105 us  [exchange(): pl.pallas_call(exchange_kernel, name='exchange', out_shape=(big,) * 7 + (...]
where the time goes in v5:
time: 127 us; the launch traced here: 126 us
  Pallas kernels  121 us (95%)
  local copies, waits for them, and re-layouts  2.47 us (2%)
    pallas_call x1, Pallas kernels, exchange(): pl.pallas_call(exchange_kernel, name='exchange', out_shape=(big,) * 7 + (...  105 us
    pallas_call x1, Pallas kernels, parent_out(): pl.pallas_call(parent_kernel, name='parent_out', out_shape=jax.ShapeDtype...  16 us

profile of v5, /device:TPU:95, one launch (start us, length us, event | category | flops | bytes accessed | tf_op | source)
XLA Modules:
  0.0 125.5 jit_solution(1844477977872631864)
XLA Ops:
  0.6 0.6 pad_add_fusion.at
  1.2 1.2 pad.4.cmap
  2.4 105.2 %exchange.1 = (bf16[16,512,128]{2,1,0:T(8,128)(2,1)}, bf16[16,512,128]{2,1,0:T(8,128)(2,1)}, bf16[16,512,128]{2,1,0:T(8,128)(2,1)}, bf16[16,512,128]{2,1,0:T(8,1...) custom-call(bf16[32,512,128]{2,1,0:T(8,128)(2,1)} %bitcast.24, ...), custom_call_target="tpu_custom_call" | custom-call | flops 67108864 | bytes 41943040 | tf_op jit(solution)/shard_map/exchange/pallas_call | solution.py:428
  107.6 0.7 fusion
  108.3 0.6 reshape.28.src
  108.9 0.0 copy-start
  108.9 16.0 %parent_out.1 = f32[16,512,128]{2,1,0:T(8,128)} custom-call(s32[128]{0:T(128)} %reshape.28.src, s32[4]{0:T(128)} %pad_add_fusion.at, bf16[32,512,128]{2,1,0:T(8,128)(2,1)} %bitcast.25, bf16[16,512,128]{2,1,0:T(8,128)(2,1)} %get-tuple-element.15.refs_1_.refs_9_.refs_17_.refs_25_, bf16[16,512,128]{2,1,0:T(8,128)(2,1)} %get-tuple-element.16.refs_2_.refs_10_.refs_18_.refs_26_, ...), custom_call_target="tpu_custom_call" | custom-call | flops 2147483648 | bytes 14680064 | tf_op jit(solution)/shard_map/parent_out/pallas_call | solution.py:543
  124.8 0.0 copy-done
  124.8 0.7 copy.8
Async XLA Ops:
  108.9 16.0 %copy-start = (f32[2,16,16,128]{3,2,1,0:T(8,128)S(1)}, f32[2,16,16,128]{3,2,1,0:T(8,128)}, u32[]{:S(2)}) copy-start(f32[2,16,16,128]{3,2,1,0:T(8,128)} %get-tuple-element.13) | copy-start | bytes 786436
